TPU v7x, 512 devices: a whole 4x4x16 slice. The times are simulated.
512 devices in a mesh: cam: 32 (over z, x_lo), row: 16 (over y, x_hi, core).
Axes of the slice: x: 4 (x_hi: 2, x_lo: 2; x = x_hi * 2 + x_lo), y: 4, z: 16, core: 2. Of those that a mesh axis runs over, the one named last changes fastest.
Arguments:
- features_in: bfloat16 [32, 64, 128, 128], P('cam', 'row'), may hold values from -6 to 6
- conv_weight: bfloat16 [3, 3, 128, 128], replicated, may hold values from -0.1875 to 0.1875
- q_weight: bfloat16 [128, 128], replicated, may hold values from -0.5 to 0.5
- k_weight: bfloat16 [128, 128], replicated, may hold values from -0.5 to 0.5
- v_weight: bfloat16 [128, 128], replicated, may hold values from -0.5 to 0.5
- partners: int32 [32, 2], replicated, may hold values from 0 to 31, as said below
- band_widths: int32 [32, 2], replicated, may hold values from 1 to 3, as said below
- bands: int32 [32, 64, 2, 3], P('cam', 'row'), may hold values from 0 to 63, as said below
- grad_attended: bfloat16 [32, 64, 128, 128], P('cam', 'row'), may hold values from -6 to 6
Outputs:
- attended: bfloat16 [32, 64, 128, 128], P('cam', 'row')
- grad_features: bfloat16 [32, 64, 128, 128], P('cam', 'row')
Inputs may be any that keep to these rules, and one draw needn't show every extreme that they name: `partners`: view c is camera c // 2 of sample c % 2; partner 0 of view c is view c - 2 or c - 4 and partner 1 is view c + 2 or c + 4, modulo 32, so both are cameras of the same sample next or next but one in the cyclic order of its 16 cameras. `band_widths`: some view and partner have 3 live slots and some have 1. `bands`: entries are block numbers of the partner view; a block is one image row, so the block number is the image row; the 3 entries of a list are distinct and lie in image rows 4 * s - 2 to 4 * (s + 1) + 1, where s is the query block's image row // 4.
All inputs are finite; a program needn't handle non-finite values.
Results may differ from a plain program's by a relative error of at most 0.011.
Values may be sent and summed in bfloat16 or wider, within the bound.
A program may use at most 64 MiB of HBM per device.

v0:
```python
import jax
import jax.numpy as jnp
from jax import lax
from jax.sharding import PartitionSpec as P

BLOCK = 128
MARGIN = 2
BAND = 3


def from_behind(value, axis, steps):
    count = lax.axis_size(axis)
    pairs = [(source, (source + steps) % count) for source in range(count)]
    return lax.ppermute(value, axis, pairs)


def passed_along(block, axis, distance):
    devices = range(lax.axis_size(axis))
    route = [(i - distance, i) for i in devices if i - distance in devices]
    return lax.ppermute(block, axis, route)


def padded_2(shard, sides, width):
    for axis, dim in sides:
        peers, length = (lax.axis_size(axis), shard.shape[dim])
        up = [(i, (i + 1) % peers) for i in range(peers - 1)]
        down = [(j, i) for i, j in up]
        last = lax.slice_in_dim(shard, length - width, length, axis=dim)
        leading = lax.slice_in_dim(shard, 0, width, axis=dim)
        before = lax.ppermute(last, axis, up)
        after = lax.ppermute(leading, axis, down)
        shard = jnp.concatenate([before, shard, after], axis=dim)
    return shard


def conv_slab(padded, conv_weight, out_rows):
    img_width = padded.shape[1]
    channels = padded.shape[2]
    side_zero = jnp.zeros((padded.shape[0], 1, channels), padded.dtype)
    framed = jnp.concatenate([side_zero, padded, side_zero], axis=1)
    total = jnp.zeros((out_rows * img_width, conv_weight.shape[3]), jnp.float32)
    for row_off in range(3):
        for col_off in range(3):
            patch = framed[row_off : row_off + out_rows, col_off : col_off + img_width].reshape(
                out_rows * img_width, channels
            )
            total = total + jnp.dot(
                patch, conv_weight[row_off, col_off], preferred_element_type=jnp.float32
            )
    return total.astype(jnp.bfloat16)


def offsets_of(partners, camera, views):
    pair_row = lax.dynamic_index_in_dim(partners, jnp.mod(camera, views), 0, keepdims=False)
    return (jnp.mod(camera - pair_row[0], views), jnp.mod(pair_row[1] - camera, views))


def view_shift(window, step_by):
    return from_behind(window, "cam", step_by)


def send_back(window, step_by):
    return from_behind(window.astype(jnp.bfloat16), "cam", step_by).astype(window.dtype)


def row_back(window, step_by):
    return passed_along(window.astype(jnp.bfloat16), "row", step_by).astype(window.dtype)


def local(
    features_in,
    conv_weight,
    q_weight,
    k_weight,
    v_weight,
    partners,
    band_widths,
    bands,
    grad_attended,
):
    image = features_in[0]
    slab_rows = image.shape[0]
    img_width = image.shape[1]
    channels = image.shape[2]
    margin_rows = MARGIN
    per_row = img_width // BLOCK
    win_rows = slab_rows + 2 * margin_rows
    high = lax.Precision.HIGHEST
    kv_weight = jnp.concatenate([k_weight, v_weight], axis=1)
    padded = padded_2(image, (("row", 0),), 1)
    hidden = conv_slab(padded, conv_weight, slab_rows)
    kv_own = jnp.dot(hidden, kv_weight, preferred_element_type=jnp.float32).astype(jnp.bfloat16)
    kv_own = kv_own.reshape(slab_rows, img_width, 2 * channels)
    kv_window = padded_2(kv_own, (("row", 0),), margin_rows)
    queries = jnp.dot(hidden, q_weight, preferred_element_type=jnp.float32).astype(jnp.bfloat16)
    views = lax.axis_size("cam")
    samples = views // min(16, views)
    camera = lax.axis_index("cam")
    slab = lax.axis_index("row")
    before, after = offsets_of(partners, camera, views)
    near_left = view_shift(kv_window, samples)
    far_left = view_shift(kv_window, 2 * samples)
    near_right = view_shift(kv_window, -samples)
    far_right = view_shift(kv_window, -2 * samples)
    left_win = jnp.where(before == samples, near_left, far_left)
    right_win = jnp.where(after == samples, near_right, far_right)
    q_blocks_dev = slab_rows * per_row
    win_blocks = win_rows * per_row
    key_count = 2 * BAND * BLOCK
    local_ids = bands[0] - per_row * (slab * slab_rows - margin_rows)

    def pick_blocks(window, side_idx):
        return jnp.take(window, local_ids[:, side_idx, :], axis=0)

    chosen = jnp.concatenate([pick_blocks(left_win, 0), pick_blocks(right_win, 1)], axis=1)
    chosen = chosen.reshape(q_blocks_dev, key_count, 2 * channels)
    key_rows = chosen[:, :, :channels]
    value_rows = chosen[:, :, channels:]
    widths_here = lax.dynamic_index_in_dim(band_widths, camera, 0, keepdims=False)
    slots = jnp.arange(BAND, dtype=jnp.int32)
    live = jnp.repeat(jnp.concatenate([slots < widths_here[0], slots < widths_here[1]]), BLOCK)
    inverse_square_root = channels ** (-0.5)
    query_block = queries.reshape(q_blocks_dev, BLOCK, channels)
    score_matrix = (
        jnp.einsum("apx,anx->apn", query_block, key_rows, preferred_element_type=jnp.float32)
        * inverse_square_root
    )
    expo = jnp.where(live, jnp.exp(score_matrix), 0.0)
    probs = expo / jnp.sum(expo, axis=2, keepdims=True)
    probabilities_halfwidth = probs.astype(jnp.bfloat16)
    attended = jnp.einsum(
        "zld,zdi->zli", probabilities_halfwidth, value_rows, preferred_element_type=jnp.float32
    ).astype(jnp.bfloat16)
    incoming_gradient = grad_attended[0]
    probability_gradient = jnp.einsum(
        "apx,anx->apn", incoming_gradient, value_rows, preferred_element_type=jnp.float32
    )
    delta = jnp.sum(probs * probability_gradient, axis=2, keepdims=True)
    score_gradient = (probs * (probability_gradient - delta)).astype(jnp.bfloat16)
    query_gradient = (
        jnp.einsum("zld,zdi->zli", score_gradient, key_rows, preferred_element_type=jnp.float32)
        * inverse_square_root
    )
    key_gradient = (
        jnp.einsum("wds,wdm->wsm", score_gradient, query_block, preferred_element_type=jnp.float32)
        * inverse_square_root
    )
    value_gradient = jnp.einsum(
        "wds,wdm->wsm",
        probabilities_halfwidth,
        incoming_gradient,
        preferred_element_type=jnp.float32,
    )
    grad_pairs = jnp.concatenate([key_gradient, value_gradient], axis=2).reshape(
        q_blocks_dev, 2, BAND, BLOCK, 2 * channels
    )
    back_weight = kv_weight.astype(jnp.float32).T

    def window_grad(side_idx):
        summed = (
            jnp.zeros((win_blocks, BLOCK, 2 * channels), jnp.float32)
            .at[local_ids[:, side_idx, :]]
            .add(grad_pairs[:, side_idx])
        )
        projected = jnp.dot(
            summed.reshape(win_rows * img_width, 2 * channels), back_weight, precision=high
        )
        return projected.reshape(win_rows, img_width, channels)

    grad_left = window_grad(0)
    grad_right = window_grad(1)
    window_total = jnp.zeros_like(grad_left)
    for distance in (1, 2):
        step_by = distance * samples
        window_total = window_total + send_back(
            jnp.where(before == step_by, grad_left, 0.0), -step_by
        )
        window_total = window_total + send_back(
            jnp.where(after == step_by, grad_right, 0.0), step_by
        )
    center = window_total[margin_rows : margin_rows + slab_rows]
    lower_in = row_back(window_total[:margin_rows], -1)
    upper_in = row_back(window_total[margin_rows + slab_rows :], 1)
    center = center.at[slab_rows - margin_rows :].add(lower_in)
    center = center.at[:margin_rows].add(upper_in)
    grad_own = jnp.dot(
        query_gradient.reshape(-1, channels), q_weight.astype(jnp.float32).T, precision=high
    )
    grad_features = (grad_own.reshape(slab_rows, img_width, channels) + center).astype(jnp.bfloat16)
    return (attended[None], grad_features[None])


def solution(mesh):
    placed = (
        P("cam", "row", None, None),
        P(),
        P(),
        P(),
        P(),
        P(),
        P(),
        P("cam", "row", None, None),
        P("cam", "row", None, None),
    )
    return jax.shard_map(
        local,
        mesh=mesh,
        in_specs=placed,
        out_specs=(P("cam", "row", None, None), P("cam", "row", None, None)),
        check_vma=False,
    )
```

profile of v0, /device:TPU:10, one launch (start us, length us, event | category | flops | bytes accessed | tf_op | source)
XLA Modules:
  0.0 146.1 jit_solution(7555800941441037937)
XLA Ops:
  0.7 0.8 slice_bitcast_fusion.1
  1.5 1.9 %collective-permute-start = (bf16[1,128,128]{2,1,0:T(8,128)(2,1)S(1)}, bf16[1,128,128]{2,1,0:T(8,128)(2,1)S(1)}, u32[]{:S(2)}, u32[]{:S(2)}) collective-permute-start(bf16[1,128,128]{2,1,0:T(8,128)(2,1)S(1)} %get-tuple-element.47), channel_id=1, source_target_pairs={{0,1},{1,2},{2,3},{3,4},{4,5},{5,6},{6,7},{7,8},{8,9},{9,10},{10,1... | collective-permute-start | bytes 98312 | tf_op jit(solution)/shard_map/ppermute | solution.py:30
  3.4 6.0 %collective-permute-start.1 = (bf16[1,128,128]{2,1,0:T(8,128)(2,1)S(1)}, bf16[1,128,128]{2,1,0:T(8,128)(2,1)S(1)}, u32[]{:S(2)}, u32[]{:S(2)}) collective-permute-start(bf16[1,128,128]{2,1,0:T(8,128)(2,1)S(1)} %get-tuple-element.48), channel_id=1, source_target_pairs={{1,0},{2,1},{3,2},{4,3},{5,4},{6,5},{7,6},{8,7},{9,8},{10,9},{11,1... | collective-permute-start | bytes 98312 | tf_op jit(solution)/shard_map/ppermute | solution.py:31
  9.5 0.7 subtract_bitcast_fusion
  10.4 0.8 constant_dynamic-slice_fusion.1
  11.2 0.5 fusion.52
  11.8 0.8 constant_dynamic-update-slice_fusion.1
  12.6 0.7 constant_dynamic-slice_fusion
  13.3 0.8 constant_dynamic-update-slice_fusion
  14.1 1.3 iota_compare_fusion
  15.4 0.9 pad_maximum_fusion.3
  16.3 0.2 pad_slice_fusion.3
  16.5 0.2 fusion.27
  16.9 0.2 convolution_add_fusion.7
  17.1 0.2 convolution_add_fusion.6
  17.3 0.2 convolution_add_fusion.5
  17.4 0.2 convolution_add_fusion.4
  17.6 0.2 convolution_add_fusion.3
  17.8 0.2 convolution_add_fusion.2
  18.0 0.2 fusion.4
  18.2 0.2 convolution_convert_fusion
  18.4 1.9 %collective-permute-start.3 = (bf16[2,128,256]{2,1,0:T(8,128)(2,1)S(1)}, bf16[2,128,256]{2,1,0:T(8,128)(2,1)S(1)}, u32[]{:S(2)}, u32[]{:S(2)}) collective-permute-start(bf16[2,128,256]{2,1,0:T(8,128)(2,1)S(1)} %bitcast.149), channel_id=1, source_target_pairs={{1,0},{2,1},{3,2},{4,3},{5,4},{6,5},{7,6},{8,7},{9,8},{10,9},{11,1... | collective-permute-start | bytes 393224 | tf_op jit(solution)/shard_map/ppermute | solution.py:31
  20.4 2.4 %collective-permute-start.2 = (bf16[2,128,256]{2,1,0:T(8,128)(2,1)S(1)}, bf16[2,128,256]{2,1,0:T(8,128)(2,1)S(1)}, u32[]{:S(2)}, u32[]{:S(2)}) collective-permute-start(bf16[2,128,256]{2,1,0:T(8,128)(2,1)S(1)} %bitcast.148), channel_id=1, source_target_pairs={{0,1},{1,2},{2,3},{3,4},{4,5},{5,6},{6,7},{7,8},{8,9},{9,10},{10,1... | collective-permute-start | bytes 393224 | tf_op jit(solution)/shard_map/ppermute | solution.py:30
  22.9 0.5 fusion.53
  23.4 5.6 %collective-permute-done.2 = bf16[2,128,256]{2,1,0:T(8,128)(2,1)S(1)} collective-permute-done((bf16[2,128,256]{2,1,0:T(8,128)(2,1)S(1)}, bf16[2,128,256]{2,1,0:T(8,128)(2,1)S(1)}, u32[]{:S(2)}, u32[]{:S(2)}) %collective-permute-start.2) | collective-permute-done | bytes 131104 | tf_op jit(solution)/shard_map/ppermute | solution.py:30
  29.1 11.9 %collective-permute-start.7 = (bf16[8,128,256]{2,1,0:T(8,128)(2,1)S(1)}, bf16[8,128,256]{2,1,0:T(8,128)(2,1)S(1)}, u32[]{:S(2)}, u32[]{:S(2)}) collective-permute-start(bf16[8,128,256]{2,1,0:T(8,128)(2,1)S(1)} %pad_maximum_fusion.2), channel_id=1, source_target_pairs={{0,448},{16,464},{32,480},{48,496},{64,0},{80,16},{96,32},{112,48}... | collective-permute-start | bytes 1572872 | tf_op jit(solution)/shard_map/ppermute | solution.py:14
  41.0 2.9 %collective-permute-start.6 = (bf16[8,128,256]{2,1,0:T(8,128)(2,1)S(1)}, bf16[8,128,256]{2,1,0:T(8,128)(2,1)}, u32[]{:S(2)}, u32[]{:S(2)}) collective-permute-start(bf16[8,128,256]{2,1,0:T(8,128)(2,1)S(1)} %pad_maximum_fusion.2), channel_id=1, source_target_pairs={{0,480},{16,496},{32,0},{48,16},{64,32},{80,48},{96,64},{112,80},{... | collective-permute-start | bytes 1572872 | tf_op jit(solution)/shard_map/ppermute | solution.py:14
  44.0 3.4 %collective-permute-start.5 = (bf16[8,128,256]{2,1,0:T(8,128)(2,1)S(1)}, bf16[8,128,256]{2,1,0:T(8,128)(2,1)S(1)}, u32[]{:S(2)}, u32[]{:S(2)}) collective-permute-start(bf16[8,128,256]{2,1,0:T(8,128)(2,1)S(1)} %pad_maximum_fusion.2), channel_id=1, source_target_pairs={{0,64},{16,80},{32,96},{48,112},{64,128},{80,144},{96,160},{112,17... | collective-permute-start | bytes 1572872 | tf_op jit(solution)/shard_map/ppermute | solution.py:14
  47.3 1.9 %collective-permute-start.4 = (bf16[8,128,256]{2,1,0:T(8,128)(2,1)S(1)}, bf16[8,128,256]{2,1,0:T(8,128)(2,1)S(1)}, u32[]{:S(2)}, u32[]{:S(2)}) collective-permute-start(bf16[8,128,256]{2,1,0:T(8,128)(2,1)S(1)} %pad_maximum_fusion.2), channel_id=1, source_target_pairs={{0,32},{16,48},{32,64},{48,80},{64,96},{80,112},{96,128},{112,144}... | collective-permute-start | bytes 1572872 | tf_op jit(solution)/shard_map/ppermute | solution.py:14
  50.9 0.2 convolution_convert_fusion.1
  51.1 10.8 %collective-permute-done.7 = bf16[8,128,256]{2,1,0:T(8,128)(2,1)S(1)} collective-permute-done((bf16[8,128,256]{2,1,0:T(8,128)(2,1)S(1)}, bf16[8,128,256]{2,1,0:T(8,128)(2,1)S(1)}, u32[]{:S(2)}, u32[]{:S(2)}) %collective-permute-start.7) | collective-permute-done | bytes 524320 | tf_op jit(solution)/shard_map/ppermute | solution.py:14
  61.9 9.4 %collective-permute-done.6 = bf16[8,128,256]{2,1,0:T(8,128)(2,1)} collective-permute-done((bf16[8,128,256]{2,1,0:T(8,128)(2,1)S(1)}, bf16[8,128,256]{2,1,0:T(8,128)(2,1)}, u32[]{:S(2)}, u32[]{:S(2)}) %collective-permute-start.6) | collective-permute-done | bytes 524320 | tf_op jit(solution)/shard_map/ppermute | solution.py:14
  71.3 1.1 broadcast_select_fusion.2
  72.4 0.6 gather_fusion.1
  73.0 6.8 %collective-permute-done.4 = bf16[8,128,256]{2,1,0:T(8,128)(2,1)S(1)} collective-permute-done((bf16[8,128,256]{2,1,0:T(8,128)(2,1)S(1)}, bf16[8,128,256]{2,1,0:T(8,128)(2,1)S(1)}, u32[]{:S(2)}, u32[]{:S(2)}) %collective-permute-start.4) | collective-permute-done | bytes 524320 | tf_op jit(solution)/shard_map/ppermute | solution.py:14
  79.8 0.6 gather_fusion
  80.4 0.2 broadcast_select_fusion
  80.8 1.7 %fusion.10 = f32[4,768,128]{1,2,0:T(8,128)} fusion(bf16[4,768,256]{2,1,0:T(8,128)(2,1)S(1)} %bitcast.126, bf16[1,4,128,128]{3,2,1,0:T(8,128)(2,1)S(1)} %copy-done), kind=kOutput, calls=%fused_computation.34 | convolution fusion | flops 100663296 | bytes 2490368 | tf_op jit(solution)/shard_map/apx,anx->apn/dot_general | solution.py:135
  82.5 2.2 %fusion = (f32[4,128]{1,0:T(4,128)S(1)}, f32[4,128,768]{2,1,0:T(8,128)S(1)}) fusion(f32[4,768,128]{1,2,0:T(8,128)} %fusion.10, bf16[4,128,128]{2,1,0:T(8,128)(2,1)S(1)} %bitcast.139, pred[768]{0:T(1024)(128)(4,1)S(1)} %broadcast_bitcast_fusion, bf16[4,768,256]{2,1,0:T(8,128)(2,1)S(1)} %bitcast.127), kind=kOutput, calls=%fused_computation.8 | convolution fusion | flops 102630144 | bytes 4066304 | tf_op jit(solution)/shard_map/div | solution.py:129
  84.7 0.4 fusion.15
  85.1 1.0 copy-done.3
  86.1 0.2 fusion.2
  86.3 0.7 copy-done.7
  87.0 0.4 convolution_multiply_fusion
  87.4 1.9 %pad_maximum_fusion = f32[4,768,256]{1,2,0:T(8,128)} fusion(f32[4,768,128]{1,2,0:T(8,128)S(1)} %fusion.15, f32[4,768,128]{1,2,0:T(8,128)S(1)} %convolution_multiply_fusion), kind=kLoop, calls=%fused_computation.4 | loop fusion | flops 786432 | bytes 6291456 | tf_op jit(solution)/shard_map/concatenate | solution.py:154
  89.3 3.5 %copy.26 = f32[4,768,256]{2,1,0:T(8,128)} copy(f32[4,768,256]{1,2,0:T(8,128)} %pad_maximum_fusion) | data formatting | bytes 6291456 | tf_op jit(solution)/shard_map/concatenate | solution.py:154
  92.8 3.9 %fusion.48 = (f32[4,1,3,128,256]{4,3,2,1,0:T(8,128)}, f32[4,1,3,128,256]{4,3,2,1,0:T(8,128)}) fusion(f32[4,2,3,128,256]{4,3,2,1,0:T(8,128)} %bitcast.125), kind=kLoop, calls=%fused_computation.110 | loop fusion | bytes 6291456 | tf_op jit(solution)/shard_map/slice | solution.py:163
  96.8 3.1 %scatter_fusion.1 = f32[8,128,256]{2,1,0:T(8,128)S(1)} fusion(f32[8,128,256]{2,1,0:T(8,128)S(1)} %broadcast.99.clone, s32[12]{0:T(128)S(1)} %reshape.231, f32[12,128,256]{2,1,0:T(8,128)} %bitcast.131), kind=kCustom, calls=%fused_computation.3 | custom fusion | flops 393216 | bytes 4718640 | tf_op jit(solution)/shard_map/scatter-add | solution.py:163
  99.9 2.3 %select_convert_fusion.2 = (bf16[8,128,128]{2,1,0:T(8,128)(2,1)}, bf16[8,128,128]{2,1,0:T(8,128)(2,1)}) fusion(pred[]{:T(512)S(6)} %eq.19, pred[]{:T(512)S(6)} %eq.21, f32[8,128,256]{2,1,0:T(8,128)S(1)} %scatter_fusion.1, bf16[128,256]{1,0:T(8,128)(2,1)} %copy-done.5), kind=kOutput, calls=%fused_computation.43 | convolution fusion | flops 402915328 | bytes 1638402 | tf_op jit(solution)/shard_map/dot_general | solution.py:165
  102.2 1.9 %collective-permute-start.9 = (bf16[8,128,128]{2,1,0:T(8,128)(2,1)}, bf16[8,128,128]{2,1,0:T(8,128)(2,1)}, u32[]{:S(2)}, u32[]{:S(2)}) collective-permute-start(bf16[8,128,128]{2,1,0:T(8,128)(2,1)} %get-tuple-element.35), channel_id=1, source_target_pairs={{0,32},{16,48},{32,64},{48,80},{64,96},{80,112},{96,128},{112,144}... | collective-permute-start | bytes 786440 | tf_op jit(solution)/shard_map/ppermute | solution.py:14
  104.1 2.1 %collective-permute-start.11 = (bf16[8,128,128]{2,1,0:T(8,128)(2,1)}, bf16[8,128,128]{2,1,0:T(8,128)(2,1)}, u32[]{:S(2)}, u32[]{:S(2)}) collective-permute-start(bf16[8,128,128]{2,1,0:T(8,128)(2,1)} %get-tuple-element.36), channel_id=1, source_target_pairs={{0,64},{16,80},{32,96},{48,112},{64,128},{80,144},{96,160},{112,17... | collective-permute-start | bytes 786440 | tf_op jit(solution)/shard_map/ppermute | solution.py:14
  106.3 3.1 %scatter_fusion = f32[8,128,256]{2,1,0:T(8,128)S(1)} fusion(f32[8,128,256]{2,1,0:T(8,128)S(1)} %broadcast.99.clone.1, s32[12]{0:T(128)S(1)} %reshape.223, f32[12,128,256]{2,1,0:T(8,128)} %bitcast.130), kind=kCustom, calls=%fused_computation.2 | custom fusion | flops 393216 | bytes 4718640 | tf_op jit(solution)/shard_map/scatter-add | solution.py:163
  109.4 1.6 %select_convert_fusion.3 = (bf16[8,128,128]{2,1,0:T(8,128)(2,1)S(1)}, bf16[8,128,128]{2,1,0:T(8,128)(2,1)S(1)}) fusion(pred[]{:T(512)S(6)} %eq.18, pred[]{:T(512)S(6)} %eq.20, f32[8,128,256]{2,1,0:T(8,128)S(1)} %scatter_fusion, bf16[128,256]{1,0:T(8,128)(2,1)} %copy-done.5), kind=kOutput, calls=%fused_computation.44 | convolution fusion | flops 402915328 | bytes 1638402 | tf_op jit(solution)/shard_map/dot_general | solution.py:165
  111.0 5.0 %collective-permute-start.8 = (bf16[8,128,128]{2,1,0:T(8,128)(2,1)S(1)}, bf16[8,128,128]{2,1,0:T(8,128)(2,1)S(1)}, u32[]{:S(2)}, u32[]{:S(2)}) collective-permute-start(bf16[8,128,128]{2,1,0:T(8,128)(2,1)S(1)} %get-tuple-element.33), channel_id=1, source_target_pairs={{0,480},{16,496},{32,0},{48,16},{64,32},{80,48},{96,64},{112,80},{... | collective-permute-start | bytes 786440 | tf_op jit(solution)/shard_map/ppermute | solution.py:14
  116.0 4.8 %collective-permute-start.10 = (bf16[8,128,128]{2,1,0:T(8,128)(2,1)S(1)}, bf16[8,128,128]{2,1,0:T(8,128)(2,1)S(1)}, u32[]{:S(2)}, u32[]{:S(2)}) collective-permute-start(bf16[8,128,128]{2,1,0:T(8,128)(2,1)S(1)} %get-tuple-element.34), channel_id=1, source_target_pairs={{0,448},{16,464},{32,480},{48,496},{64,0},{80,16},{96,32},{112,48}... | collective-permute-start | bytes 786440 | tf_op jit(solution)/shard_map/ppermute | solution.py:14
  120.8 0.4 convolution_multiply_fusion.1
  121.2 5.9 %collective-permute-done.8 = bf16[8,128,128]{2,1,0:T(8,128)(2,1)S(1)} collective-permute-done((bf16[8,128,128]{2,1,0:T(8,128)(2,1)S(1)}, bf16[8,128,128]{2,1,0:T(8,128)(2,1)S(1)}, u32[]{:S(2)}, u32[]{:S(2)}) %collective-permute-start.8) | collective-permute-done | bytes 262176 | tf_op jit(solution)/shard_map/ppermute | solution.py:14
  127.1 3.9 %collective-permute-done.10 = bf16[8,128,128]{2,1,0:T(8,128)(2,1)S(1)} collective-permute-done((bf16[8,128,128]{2,1,0:T(8,128)(2,1)S(1)}, bf16[8,128,128]{2,1,0:T(8,128)(2,1)S(1)}, u32[]{:S(2)}, u32[]{:S(2)}) %collective-permute-start.10) | collective-permute-done | bytes 262176 | tf_op jit(solution)/shard_map/ppermute | solution.py:14
  131.0 1.2 fusion.47
  132.2 3.9 %collective-permute-start.12 = (bf16[2,128,128]{2,1,0:T(8,128)(2,1)S(1)}, bf16[2,128,128]{2,1,0:T(8,128)(2,1)S(1)}, u32[]{:S(2)}, u32[]{:S(2)}) collective-permute-start(bf16[2,128,128]{2,1,0:T(8,128)(2,1)S(1)} %get-tuple-element.32), channel_id=1, source_target_pairs={{1,0},{2,1},{3,2},{4,3},{5,4},{6,5},{7,6},{8,7},{9,8},{10,9},{11,1... | collective-permute-start | bytes 196616 | tf_op jit(solution)/shard_map/ppermute | solution.py:20
  136.1 1.0 fusion.7
  137.2 1.9 %collective-permute-start.13 = (bf16[2,128,128]{2,1,0:T(8,128)(2,1)S(1)}, bf16[2,128,128]{2,1,0:T(8,128)(2,1)S(1)}, u32[]{:S(2)}, u32[]{:S(2)}) collective-permute-start(bf16[2,128,128]{2,1,0:T(8,128)(2,1)S(1)} %get-tuple-element.31), channel_id=1, source_target_pairs={{0,1},{1,2},{2,3},{3,4},{4,5},{5,6},{6,7},{7,8},{8,9},{9,10},{10,1... | collective-permute-start | bytes 196616 | tf_op jit(solution)/shard_map/ppermute | solution.py:20
  139.1 6.0 %collective-permute-done.13 = bf16[2,128,128]{2,1,0:T(8,128)(2,1)S(1)} collective-permute-done((bf16[2,128,128]{2,1,0:T(8,128)(2,1)S(1)}, bf16[2,128,128]{2,1,0:T(8,128)(2,1)S(1)}, u32[]{:S(2)}, u32[]{:S(2)}) %collective-permute-start.13) | collective-permute-done | bytes 65568 | tf_op jit(solution)/shard_map/ppermute | solution.py:20
  145.2 0.9 fusion.6
  (57 shorter events, 1.7 us)
Async XLA Ops:
  0.6 80.2 %copy-start = (bf16[1,4,128,128]{3,2,1,0:T(8,128)(2,1)S(1)}, bf16[1,4,128,128]{3,2,1,0:T(8,128)(2,1)}, u32[]{:S(2)}) copy-start(bf16[1,4,128,128]{3,2,1,0:T(8,128)(2,1)} %param.23) | copy-start | bytes 393220
  0.6 16.2 %copy-start.4 = (bf16[1,4,128,128]{3,2,1,0:T(8,128)(2,1)S(1)}, bf16[1,4,128,128]{3,2,1,0:T(8,128)(2,1)}, u32[]{:S(2)}) copy-start(bf16[1,4,128,128]{3,2,1,0:T(8,128)(2,1)} %param.15) | copy-start | bytes 393220
  0.7 15.9 %copy-start.8 = (bf16[3,3,128,128]{3,2,1,0:T(8,128)(2,1)S(1)}, bf16[3,3,128,128]{3,2,1,0:T(8,128)(2,1)}, u32[]{:S(2)}) copy-start(bf16[3,3,128,128]{3,2,1,0:T(8,128)(2,1)} %param.16) | copy-start | bytes 884740
  1.5 13.9 %collective-permute-start = (bf16[1,128,128]{2,1,0:T(8,128)(2,1)S(1)}, bf16[1,128,128]{2,1,0:T(8,128)(2,1)S(1)}, u32[]{:S(2)}, u32[]{:S(2)}) collective-permute-start(bf16[1,128,128]{2,1,0:T(8,128)(2,1)S(1)} %get-tuple-element.47), channel_id=1, source_target_pairs={{0,1},{1,2},{2,3},{3,4},{4,5},{5,6},{6,7},{7,8},{8,9},{9,10},{10,1... | collective-permute-start | bytes 98312 | tf_op jit(solution)/shard_map/ppermute | solution.py:30
  3.4 12.0 %collective-permute-start.1 = (bf16[1,128,128]{2,1,0:T(8,128)(2,1)S(1)}, bf16[1,128,128]{2,1,0:T(8,128)(2,1)S(1)}, u32[]{:S(2)}, u32[]{:S(2)}) collective-permute-start(bf16[1,128,128]{2,1,0:T(8,128)(2,1)S(1)} %get-tuple-element.48), channel_id=1, source_target_pairs={{1,0},{2,1},{3,2},{4,3},{5,4},{6,5},{7,6},{8,7},{9,8},{10,9},{11,1... | collective-permute-start | bytes 98312 | tf_op jit(solution)/shard_map/ppermute | solution.py:31
  14.1 4.1 %copy-start.5 = (bf16[128,256]{1,0:T(8,128)(2,1)}, bf16[128,256]{1,0:T(8,128)(2,1)S(1)}, u32[]{:S(2)}) copy-start(bf16[128,256]{1,0:T(8,128)(2,1)S(1)} %constant_dynamic-update-slice_fusion) | copy-start | bytes 196612
  18.0 32.9 %copy-start.9 = (bf16[128,128]{1,0:T(8,128)(2,1)S(1)}, bf16[128,128]{1,0:T(8,128)(2,1)}, u32[]{:S(2)}) copy-start(bf16[128,128]{1,0:T(8,128)(2,1)} %param.17) | copy-start | bytes 98308
  18.4 5.0 %collective-permute-start.3 = (bf16[2,128,256]{2,1,0:T(8,128)(2,1)S(1)}, bf16[2,128,256]{2,1,0:T(8,128)(2,1)S(1)}, u32[]{:S(2)}, u32[]{:S(2)}) collective-permute-start(bf16[2,128,256]{2,1,0:T(8,128)(2,1)S(1)} %bitcast.149), channel_id=1, source_target_pairs={{1,0},{2,1},{3,2},{4,3},{5,4},{6,5},{7,6},{8,7},{9,8},{10,9},{11,1... | collective-permute-start | bytes 393224 | tf_op jit(solution)/shard_map/ppermute | solution.py:31
  20.4 8.7 %collective-permute-start.2 = (bf16[2,128,256]{2,1,0:T(8,128)(2,1)S(1)}, bf16[2,128,256]{2,1,0:T(8,128)(2,1)S(1)}, u32[]{:S(2)}, u32[]{:S(2)}) collective-permute-start(bf16[2,128,256]{2,1,0:T(8,128)(2,1)S(1)} %bitcast.148), channel_id=1, source_target_pairs={{0,1},{1,2},{2,3},{3,4},{4,5},{5,6},{6,7},{7,8},{8,9},{9,10},{10,1... | collective-permute-start | bytes 393224 | tf_op jit(solution)/shard_map/ppermute | solution.py:30
  29.1 32.8 %collective-permute-start.7 = (bf16[8,128,256]{2,1,0:T(8,128)(2,1)S(1)}, bf16[8,128,256]{2,1,0:T(8,128)(2,1)S(1)}, u32[]{:S(2)}, u32[]{:S(2)}) collective-permute-start(bf16[8,128,256]{2,1,0:T(8,128)(2,1)S(1)} %pad_maximum_fusion.2), channel_id=1, source_target_pairs={{0,448},{16,464},{32,480},{48,496},{64,0},{80,16},{96,32},{112,48}... | collective-permute-start | bytes 1572872 | tf_op jit(solution)/shard_map/ppermute | solution.py:14
  41.0 30.3 %collective-permute-start.6 = (bf16[8,128,256]{2,1,0:T(8,128)(2,1)S(1)}, bf16[8,128,256]{2,1,0:T(8,128)(2,1)}, u32[]{:S(2)}, u32[]{:S(2)}) collective-permute-start(bf16[8,128,256]{2,1,0:T(8,128)(2,1)S(1)} %pad_maximum_fusion.2), channel_id=1, source_target_pairs={{0,480},{16,496},{32,0},{48,16},{64,32},{80,48},{96,64},{112,80},{... | collective-permute-start | bytes 1572872 | tf_op jit(solution)/shard_map/ppermute | solution.py:14
  44.0 29.0 %collective-permute-start.5 = (bf16[8,128,256]{2,1,0:T(8,128)(2,1)S(1)}, bf16[8,128,256]{2,1,0:T(8,128)(2,1)S(1)}, u32[]{:S(2)}, u32[]{:S(2)}) collective-permute-start(bf16[8,128,256]{2,1,0:T(8,128)(2,1)S(1)} %pad_maximum_fusion.2), channel_id=1, source_target_pairs={{0,64},{16,80},{32,96},{48,112},{64,128},{80,144},{96,160},{112,17... | collective-permute-start | bytes 1572872 | tf_op jit(solution)/shard_map/ppermute | solution.py:14
  47.3 32.4 %collective-permute-start.4 = (bf16[8,128,256]{2,1,0:T(8,128)(2,1)S(1)}, bf16[8,128,256]{2,1,0:T(8,128)(2,1)S(1)}, u32[]{:S(2)}, u32[]{:S(2)}) collective-permute-start(bf16[8,128,256]{2,1,0:T(8,128)(2,1)S(1)} %pad_maximum_fusion.2), channel_id=1, source_target_pairs={{0,32},{16,48},{32,64},{48,80},{64,96},{80,112},{96,128},{112,144}... | collective-permute-start | bytes 1572872 | tf_op jit(solution)/shard_map/ppermute | solution.py:14
  51.1 31.4 %copy-start.6 = (bf16[512,128]{1,0:T(8,128)(2,1)}, bf16[512,128]{1,0:T(8,128)(2,1)S(1)}, u32[]{:S(2)}) copy-start(bf16[512,128]{1,0:T(8,128)(2,1)S(1)} %convolution_convert_fusion.1) | copy-start | bytes 393220
  80.8 3.9 %copy-start.1 = (bf16[4,6,128,256]{3,2,1,0:T(8,128)(2,1)}, bf16[4,6,128,256]{3,2,1,0:T(8,128)(2,1)S(1)}, u32[]{:S(2)}) copy-start(bf16[4,6,128,256]{3,2,1,0:T(8,128)(2,1)S(1)} %pad_maximum_fusion.1) | copy-start | bytes 4718596
  84.7 1.4 copy-start.3
  86.1 0.9 copy-start.7
  102.2 19.0 %collective-permute-start.9 = (bf16[8,128,128]{2,1,0:T(8,128)(2,1)}, bf16[8,128,128]{2,1,0:T(8,128)(2,1)}, u32[]{:S(2)}, u32[]{:S(2)}) collective-permute-start(bf16[8,128,128]{2,1,0:T(8,128)(2,1)} %get-tuple-element.35), channel_id=1, source_target_pairs={{0,32},{16,48},{32,64},{48,80},{64,96},{80,112},{96,128},{112,144}... | collective-permute-start | bytes 786440 | tf_op jit(solution)/shard_map/ppermute | solution.py:14
  104.1 17.1 %collective-permute-start.11 = (bf16[8,128,128]{2,1,0:T(8,128)(2,1)}, bf16[8,128,128]{2,1,0:T(8,128)(2,1)}, u32[]{:S(2)}, u32[]{:S(2)}) collective-permute-start(bf16[8,128,128]{2,1,0:T(8,128)(2,1)} %get-tuple-element.36), channel_id=1, source_target_pairs={{0,64},{16,80},{32,96},{48,112},{64,128},{80,144},{96,160},{112,17... | collective-permute-start | bytes 786440 | tf_op jit(solution)/shard_map/ppermute | solution.py:14
  109.4 11.4 %copy-start.2 = (bf16[4,6,128,256]{3,2,1,0:T(8,128)(2,1)S(1)}, bf16[4,6,128,256]{3,2,1,0:T(8,128)(2,1)}, u32[]{:S(2)}) copy-start(bf16[4,6,128,256]{3,2,1,0:T(8,128)(2,1)} %copy-done.1) | copy-start | bytes 4718596
  111.0 16.1 %collective-permute-start.8 = (bf16[8,128,128]{2,1,0:T(8,128)(2,1)S(1)}, bf16[8,128,128]{2,1,0:T(8,128)(2,1)S(1)}, u32[]{:S(2)}, u32[]{:S(2)}) collective-permute-start(bf16[8,128,128]{2,1,0:T(8,128)(2,1)S(1)} %get-tuple-element.33), channel_id=1, source_target_pairs={{0,480},{16,496},{32,0},{48,16},{64,32},{80,48},{96,64},{112,80},{... | collective-permute-start | bytes 786440 | tf_op jit(solution)/shard_map/ppermute | solution.py:14
  116.0 15.0 %collective-permute-start.10 = (bf16[8,128,128]{2,1,0:T(8,128)(2,1)S(1)}, bf16[8,128,128]{2,1,0:T(8,128)(2,1)S(1)}, u32[]{:S(2)}, u32[]{:S(2)}) collective-permute-start(bf16[8,128,128]{2,1,0:T(8,128)(2,1)S(1)} %get-tuple-element.34), channel_id=1, source_target_pairs={{0,448},{16,464},{32,480},{48,496},{64,0},{80,16},{96,32},{112,48}... | collective-permute-start | bytes 786440 | tf_op jit(solution)/shard_map/ppermute | solution.py:14
  132.2 13.0 %copy-start.10 = (bf16[128,128]{1,0:T(8,128)(2,1)S(1)}, bf16[128,128]{1,0:T(8,128)(2,1)}, u32[]{:S(2)}) copy-start(bf16[128,128]{1,0:T(8,128)(2,1)} %param.17) | copy-start | bytes 98308
  132.2 6.9 %collective-permute-start.12 = (bf16[2,128,128]{2,1,0:T(8,128)(2,1)S(1)}, bf16[2,128,128]{2,1,0:T(8,128)(2,1)S(1)}, u32[]{:S(2)}, u32[]{:S(2)}) collective-permute-start(bf16[2,128,128]{2,1,0:T(8,128)(2,1)S(1)} %get-tuple-element.32), channel_id=1, source_target_pairs={{1,0},{2,1},{3,2},{4,3},{5,4},{6,5},{7,6},{8,7},{9,8},{10,9},{11,1... | collective-permute-start | bytes 196616 | tf_op jit(solution)/shard_map/ppermute | solution.py:20
  137.2 8.0 %collective-permute-start.13 = (bf16[2,128,128]{2,1,0:T(8,128)(2,1)S(1)}, bf16[2,128,128]{2,1,0:T(8,128)(2,1)S(1)}, u32[]{:S(2)}, u32[]{:S(2)}) collective-permute-start(bf16[2,128,128]{2,1,0:T(8,128)(2,1)S(1)} %get-tuple-element.31), channel_id=1, source_target_pairs={{0,1},{1,2},{2,3},{3,4},{4,5},{5,6},{6,7},{7,8},{8,9},{9,10},{10,1... | collective-permute-start | bytes 196616 | tf_op jit(solution)/shard_map/ppermute | solution.py:20
where the time goes:
time: 147 us; the launch traced here: 146 us
  starting transfers between devices  51.9 us (35%)
  waiting for transfers between devices  48.4 us (33%)
  local copies, waits for them, and re-layouts  16.4 us (11%)
  other arithmetic  14.2 us (10%)
  matrix products  12.7 us (9%)
  between operations  2.46 us (2%)
    ppermute x8, waiting for transfers between devices, from_behind(): return lax.ppermute(value, axis, pairs)  36.8 us
    ppermute x8, starting transfers between devices, from_behind(): return lax.ppermute(value, axis, pairs)  33.8 us
    ppermute x2, starting transfers between devices, padded_2(): after = lax.ppermute(leading, axis, down)  7.97 us
    scatter-add x2, other arithmetic, window_grad(): summed = jnp.zeros((win_blocks, BLOCK, 2 * channels), jnp.float32).at[loc...  6.25 us
    ppermute x2, waiting for transfers between devices, passed_along(): return lax.ppermute(block, axis, route)  6 us
    ppermute x2, starting transfers between devices, passed_along(): return lax.ppermute(block, axis, route)  5.83 us
    ppermute x2, waiting for transfers between devices, padded_2(): before = lax.ppermute(last, axis, up)  5.6 us
    ppermute x2, starting transfers between devices, padded_2(): before = lax.ppermute(last, axis, up)  4.31 us
  transfers between devices with their start and end apart: 14, of which 7 were waited for; matrix products, arithmetic and copies ran while one was open for 10% of the time, Pallas kernels for 0%

commit v1 on v0

v1 whole, which is shorter than its diff:
```python
import functools

import jax
import jax.numpy as jnp
from jax import lax
from jax.experimental import pallas as pl
from jax.experimental.pallas import tpu as pltpu
from jax.sharding import PartitionSpec as P

MESH = pl.DeviceIdType.MESH
BLOCK = 128
MARGIN = 2
BAND = 3
F32 = jnp.float32
BF16 = jnp.bfloat16

NN = (((1,), (0,)), ((), ()))
NT = (((1,), (1,)), ((), ()))
TN = (((0,), (0,)), ((), ()))


def dot(a, b, dims=NN):
    return lax.dot_general(a, b, dims, preferred_element_type=F32)


def kernel(
    views,
    slabs,
    feat,
    conv_w,
    q_w,
    k_w,
    v_w,
    partners,
    widths,
    bands,
    grad_att,
    att_out,
    grad_out,
    fbuf,
    wconv,
    wq,
    wk,
    wv,
    dabuf,
    hown,
    cand,
    wsel,
    qa,
    pd,
    att,
    own,
    acc,
    gmar,
    rmar,
    ztot,
    zin,
    gout,
    load_sem,
    halo_send,
    halo_recv,
    z_send,
    z_recv,
    m_send,
    m_recv,
    b_send,
    b_recv,
    y_send,
    y_recv,
    out_sem,
):
    step = views // min(16, views)
    rows = hown.shape[0]
    width, channels = hown.shape[1], hown.shape[2]
    cam = lax.axis_index("cam")
    slab = lax.axis_index("row")
    cam_r, cam_l = lax.rem(cam + step, views), lax.rem(cam + views - step, views)
    slab_n, slab_p = lax.rem(slab + 1, slabs), lax.rem(slab + slabs - 1, slabs)
    right, left = (cam_r, slab), (cam_l, slab)
    above, below = (cam, slab_p), (cam, slab_n)

    barrier = pltpu.get_barrier_semaphore()
    for peer in (right, left, above, below):
        pl.semaphore_signal(barrier, inc=1, device_id=peer, device_id_type=MESH)

    loads = [
        pltpu.make_async_copy(feat.at[0], fbuf.at[pl.ds(1, rows)], load_sem.at[0]),
        pltpu.make_async_copy(conv_w, wconv, load_sem.at[1]),
        pltpu.make_async_copy(grad_att.at[0], dabuf, load_sem.at[2]),
        pltpu.make_async_copy(v_w, wv, load_sem.at[3]),
        pltpu.make_async_copy(q_w, wq, load_sem.at[4]),
        pltpu.make_async_copy(k_w, wk, load_sem.at[5]),
    ]
    for load in loads:
        load.start()

    def remote(src, dst, send, recv, peer):
        return pltpu.make_async_remote_copy(
            src_ref=src, dst_ref=dst, send_sem=send, recv_sem=recv, device_id=peer, device_id_type=MESH
        )

    halo_up = remote(feat.at[0, 0], fbuf.at[rows + 1], halo_send.at[0], halo_recv.at[0], above)
    halo_down = remote(feat.at[0, rows - 1], fbuf.at[0], halo_send.at[1], halo_recv.at[1], below)

    def near(r):
        return (
            remote(hown.at[r], cand.at[0, r], z_send.at[0, r], z_recv.at[0, r], right),
            remote(hown.at[r], cand.at[2, r], z_send.at[2, r], z_recv.at[2, r], left),
        )

    def far(r):
        return (
            remote(cand.at[0, r], cand.at[1, r], z_send.at[1, r], z_recv.at[1, r], right),
            remote(cand.at[2, r], cand.at[3, r], z_send.at[3, r], z_recv.at[3, r], left),
        )

    def conv(taps):
        total = None
        for dy in range(3):
            weight = jnp.concatenate([wconv[dy, 0], wconv[dy, 1], wconv[dy, 2]], axis=1)
            part = dot(taps[dy], weight)
            total = part if total is None else total + part
        size = total.shape[0]
        pixel = lax.rem(lax.broadcasted_iota(jnp.int32, (size, channels), 0), width)
        before = pltpu.roll(total[:, :channels], 1, 0)
        after = pltpu.roll(total[:, 2 * channels :], size - 1, 0)
        out = total[:, channels : 2 * channels]
        out = out + jnp.where(pixel == 0, 0.0, before) + jnp.where(pixel == width - 1, 0.0, after)
        return out.astype(BF16)

    loads[0].wait()
    loads[1].wait()
    inner = conv([fbuf[pl.ds(1 + dy, rows - 2)].reshape((rows - 2) * width, channels) for dy in range(3)])
    hown[pl.ds(1, rows - 2)] = inner.reshape(rows - 2, width, channels)

    pl.semaphore_wait(barrier, 4)
    halo_up.start()
    halo_down.start()
    for r in range(1, rows - 1):
        for copy in near(r):
            copy.start()

    loads[2].wait()
    loads[3].wait()
    loads[4].wait()
    loads[5].wait()
    grad_v = dot(dabuf[...].reshape(rows * width, channels), wv[...], NT).astype(BF16)
    qa[:, pl.ds(width, width), :] = grad_v.reshape(rows, width, channels)
    pd[:, 2 * BAND] = jnp.zeros((rows, BLOCK, 2 * width), BF16)

    halo_up.wait_recv()
    halo_down.wait_recv()
    top = jnp.where(slab == 0, jnp.zeros((width, channels), BF16), fbuf[0])
    bottom = jnp.where(slab == slabs - 1, jnp.zeros((width, channels), BF16), fbuf[rows + 1])
    hown[0] = conv([top, fbuf[1], fbuf[2]])
    hown[rows - 1] = conv([fbuf[rows - 1], fbuf[rows], bottom])
    for r in (0, rows - 1):
        for copy in near(r):
            copy.start()
    order = [*range(1, rows - 1), 0, rows - 1]
    for r in order:
        for near_copy, far_copy in zip(near(r), far(r)):
            near_copy.wait_recv()
            far_copy.start()

    scale = channels**-0.5
    queries = dot(hown[...].reshape(rows * width, channels), wq[...]).astype(BF16)
    queries = (dot(queries, wk[...], NT) * scale).astype(BF16)
    qa[:, pl.ds(0, width), :] = queries.reshape(rows, width, channels)

    gap0 = lax.rem(cam - partners[cam, 0] + views, views)
    gap1 = lax.rem(partners[cam, 1] - cam + views, views)

    for r in order:
        for copy in far(r):
            copy.wait_recv()
        wsel[0, MARGIN + r] = jnp.where(gap0 == step, cand[0, r], cand[1, r])
        wsel[1, MARGIN + r] = jnp.where(gap1 == step, cand[2, r], cand[3, r])

    def margin(side):
        return (
            remote(
                wsel.at[side, pl.ds(MARGIN, MARGIN)],
                wsel.at[side, pl.ds(MARGIN + rows, MARGIN)],
                m_send.at[side, 0],
                m_recv.at[side, 0],
                above,
            ),
            remote(
                wsel.at[side, pl.ds(rows, MARGIN)],
                wsel.at[side, pl.ds(0, MARGIN)],
                m_send.at[side, 1],
                m_recv.at[side, 1],
                below,
            ),
        )

    margins = [*margin(0), *margin(1)]
    for copy in margins:
        copy.start()
    for copy in margins:
        copy.wait_recv()

    base = slab * rows - MARGIN

    def attend(q, carry):
        qa_here = qa[q]
        keys, exps, grads = [], [], []
        total, weighted = None, None
        for side in range(2):
            for slot in range(BAND):
                place = jnp.clip(bands[0, q, side, slot] - base, 0, rows + 2 * MARGIN - 1)
                block = wsel[side, place]
                both = dot(block, qa_here, NT)
                live = jnp.where(slot < widths[cam, side], 1.0, 0.0).astype(F32)
                expo = jnp.where(live > 0.0, jnp.exp(both[:, :width]), 0.0)
                grad = both[:, width:]
                keys.append(block)
                exps.append(expo)
                grads.append(grad)
                here = jnp.sum(expo, axis=0, keepdims=True)
                here_w = jnp.sum(expo * grad, axis=0, keepdims=True)
                total = here if total is None else total + here
                weighted = here_w if weighted is None else weighted + here_w
        inverse = 1.0 / total
        delta = weighted * inverse
        pairs = []
        for place in range(2 * BAND):
            prob = exps[place] * inverse
            score = prob * (grads[place] - delta)
            pair = jnp.concatenate([score.astype(BF16), prob.astype(BF16)], axis=1)
            pd[q, place] = pair
            pairs.append(pair)
        mixed = dot(jnp.concatenate(keys, axis=0), jnp.concatenate(pairs, axis=0), TN).astype(BF16)
        att[q] = dot(mixed[:, width:], wv[...], TN).astype(BF16)
        grad_q = (dot(mixed[:, :width], wk[...], TN) * scale).astype(BF16)
        own[q] = dot(grad_q, wq[...], NT)
        return carry

    lax.fori_loop(0, rows, attend, 0)

    att_copy = pltpu.make_async_copy(att, att_out.at[0], out_sem.at[0])
    att_copy.start()

    def place_of(q, side, row):
        place = jnp.int32(2 * BAND)
        for slot in range(BAND):
            place = jnp.where(bands[0, q, side, slot] - base == row, side * BAND + slot, place)
        return place

    def key_grads(which):
        summed = None
        for q in range(rows):
            lhs = jnp.concatenate([pd[q, place_of(q, side, row)] for side, row in which], axis=0)
            part = dot(lhs, qa[q])
            summed = part if summed is None else summed + part
        return summed.reshape(len(which), BLOCK, channels)

    upper = [(side, row) for side in range(2) for row in range(MARGIN)]
    lower = [(side, row) for side in range(2) for row in range(MARGIN + rows, 2 * MARGIN + rows)]
    gmar[...] = key_grads(upper + lower).astype(BF16).reshape(gmar.shape)
    back_up = remote(gmar.at[0], rmar.at[0], b_send.at[0], b_recv.at[0], above)
    back_down = remote(gmar.at[1], rmar.at[1], b_send.at[1], b_recv.at[1], below)
    back_up.start()
    back_down.start()
    middle = [(side, row) for side in range(2) for row in range(MARGIN, MARGIN + rows)]
    acc[...] = key_grads(middle).reshape(acc.shape)

    def totals(half):
        return (
            remote(ztot.at[0, half], zin.at[0, half], y_send.at[0, half], y_recv.at[0, half], left),
            remote(ztot.at[1, half], zin.at[1, half], y_send.at[1, half], y_recv.at[1, half], right),
        )

    def relays(half):
        return (
            remote(zin.at[0, half], zin.at[2, half], y_send.at[2, half], y_recv.at[2, half], left),
            remote(zin.at[1, half], zin.at[3, half], y_send.at[3, half], y_recv.at[3, half], right),
        )

    for half, back in ((0, back_down), (1, back_up)):
        back.wait_recv()
        for side in range(2):
            summed = acc[side, pl.ds(MARGIN * half, MARGIN)] + rmar[1 - half, side].astype(F32)
            ztot[side, half] = summed.astype(BF16)
        for copy in totals(half):
            copy.start()
    for half in range(2):
        for copy, relay in zip(totals(half), relays(half)):
            copy.wait_recv()
            relay.start()

    def gap_is(other, side, distance):
        other = lax.rem(other + 2 * views, views)
        gap = other - partners[other, 0] if side == 0 else partners[other, 1] - other
        return jnp.where(lax.rem(gap + views, views) == distance, 1, 0)

    use = (
        gap_is(cam + step, 0, step),
        gap_is(cam - step, 1, step),
        gap_is(cam + 2 * step, 0, 2 * step),
        gap_is(cam - 2 * step, 1, 2 * step),
    )
    for half in range(2):
        for copy in relays(half):
            copy.wait_recv()
        summed = own[pl.ds(MARGIN * half, MARGIN)]
        for source in range(4):
            summed = summed + jnp.where(use[source] > 0, zin[source, half].astype(F32), 0.0)
        gout[pl.ds(MARGIN * half, MARGIN)] = summed.astype(BF16)
    grad_copy = pltpu.make_async_copy(gout, grad_out.at[0], out_sem.at[1])
    grad_copy.start()

    halo_up.wait_send()
    halo_down.wait_send()
    for r in range(rows):
        for copy in (*near(r), *far(r)):
            copy.wait_send()
    for copy in margins:
        copy.wait_send()
    back_up.wait_send()
    back_down.wait_send()
    for half in range(2):
        for copy in (*totals(half), *relays(half)):
            copy.wait_send()
    att_copy.wait()
    grad_copy.wait()


def local(
    views,
    slabs,
    features_in,
    conv_weight,
    q_weight,
    k_weight,
    v_weight,
    partners,
    band_widths,
    bands,
    grad_attended,
):
    _, rows, width, channels = features_in.shape
    block = (width, channels)
    half = rows // 2
    hbm = pl.BlockSpec(memory_space=pl.ANY)
    smem = pl.BlockSpec(memory_space=pltpu.SMEM)
    dma = pltpu.SemaphoreType.DMA
    out = jax.ShapeDtypeStruct(features_in.shape, BF16)
    return pl.pallas_call(
        functools.partial(kernel, views, slabs),
        out_shape=(out, out),
        in_specs=[hbm, hbm, hbm, hbm, hbm, smem, smem, smem, hbm],
        out_specs=(hbm, hbm),
        scratch_shapes=[
            pltpu.VMEM((rows + 2, *block), BF16),
            pltpu.VMEM(conv_weight.shape, BF16),
            pltpu.VMEM(q_weight.shape, BF16),
            pltpu.VMEM(q_weight.shape, BF16),
            pltpu.VMEM(q_weight.shape, BF16),
            pltpu.VMEM((rows, *block), BF16),
            pltpu.VMEM((rows, *block), BF16),
            pltpu.VMEM((4, rows, *block), BF16),
            pltpu.VMEM((2, rows + 2 * MARGIN, *block), BF16),
            pltpu.VMEM((rows, 2 * width, channels), BF16),
            pltpu.VMEM((rows, 2 * BAND + 1, BLOCK, 2 * width), BF16),
            pltpu.VMEM((rows, *block), BF16),
            pltpu.VMEM((rows, *block), F32),
            pltpu.VMEM((2, rows, *block), F32),
            pltpu.VMEM((2, 2, MARGIN, *block), BF16),
            pltpu.VMEM((2, 2, MARGIN, *block), BF16),
            pltpu.VMEM((2, 2, half, *block), BF16),
            pltpu.VMEM((4, 2, half, *block), BF16),
            pltpu.VMEM((rows, *block), BF16),
            dma((6,)),
            dma((2,)),
            dma((2,)),
            dma((4, rows)),
            dma((4, rows)),
            dma((2, 2)),
            dma((2, 2)),
            dma((2,)),
            dma((2,)),
            dma((4, 2)),
            dma((4, 2)),
            dma((2,)),
        ],
        compiler_params=pltpu.CompilerParams(collective_id=0, has_side_effects=True),
        name="views",
    )(
        features_in,
        conv_weight,
        q_weight,
        k_weight,
        v_weight,
        partners,
        band_widths,
        bands,
        grad_attended,
    )


def solution(mesh):
    placed = (
        P("cam", "row", None, None),
        P(),
        P(),
        P(),
        P(),
        P(),
        P(),
        P("cam", "row", None, None),
        P("cam", "row", None, None),
    )
    return jax.shard_map(
        functools.partial(local, mesh.shape["cam"], mesh.shape["row"]),
        mesh=mesh,
        in_specs=placed,
        out_specs=(P("cam", "row", None, None), P("cam", "row", None, None)),
        check_vma=False,
    )
```

time: 147 us -> 56.5 us (0.38)
  the two profiles are of different devices: /device:TPU:10 before, /device:TPU:2 now
where the time goes in v1:
time: 56.5 us; the launch traced here: 56.2 us
  Pallas kernels  50.6 us (90%)
  local copies, waits for them, and re-layouts  5.02 us (9%)
  between operations  0.66 us (1%)
    pallas_call x1, Pallas kernels, local(): pl.pallas_call(functools.partial(kernel, views, slabs), out_shape=(out, o...  50.6 us
    unnamed x11, local copies, waits for them, and re-layouts  5.02 us

profile of v1, /device:TPU:2, one launch (start us, length us, event | category | flops | bytes accessed | tf_op | source)
XLA Modules:
  0.0 56.2 jit_solution(5555704940517579643)
XLA Ops:
  0.6 0.0 copy-start.1
  0.6 1.4 %copy.13.bands = s32[1,4,2,3]{3,2,1,0:T(2,128)} copy(s32[1,4,2,3]{1,2,3,0:T(2,128)} %param.16) | data formatting | bytes 192 | tf_op args[7]
  2.0 0.0 copy-done.1
  2.0 0.0 copy-start.2
  2.0 0.7 %copy.11.partners = s32[32,2]{1,0:T(8,128)} copy(s32[32,2]{0,1:T(2,128)S(1)} %copy-done.1) | data formatting | bytes 512 | tf_op args[5]
  2.7 0.0 copy-done.2
  2.7 0.7 %copy.12.widths = s32[32,2]{1,0:T(8,128)} copy(s32[32,2]{0,1:T(2,128)S(1)} %copy-done.2) | data formatting | bytes 512 | tf_op args[6]
  3.4 50.6 %views.1 = (bf16[1,4,128,128]{3,2,1,0:T(8,128)(2,1)}, bf16[1,4,128,128]{3,2,1,0:T(8,128)(2,1)}) custom-call(bf16[1,4,128,128]{3,2,1,0:T(8,128)(2,1)} %feat.1, bf16[3,3,128,128]{3,2,1,0:T(8,128)(2,1)} %conv_w.1, bf16[128,128]{1,0:T(8,128)(2,1)} %q_w.1, bf16[128,128]{1,0:T(8,128)(2,1)} %k_w.1, bf16[128,128]{1,0:T(8,128)(2,1)} %v_w.1, s32[32,2]{1,0:T(8,128)} %copy.11.partners, ...), custom_call_target="tpu_custom_call" | custom-call | tf_op jit(solution)/shard_map/views/pallas_call | solution.py:350
  54.0 0.0 copy-start
  54.0 1.6 %copy.16 = bf16[1,4,128,128]{3,2,1,0:T(8,128)(2,1)} copy(bf16[1,4,128,128]{3,2,1,0:T(8,128)(2,1)} %get-tuple-element.4) | data formatting | bytes 262144
  55.6 0.0 copy-done
  55.6 0.7 %copy.17 = bf16[1,4,128,128]{3,2,1,0:T(8,128)(2,1)} copy(bf16[1,4,128,128]{3,2,1,0:T(8,128)(2,1)S(1)} %copy-done) | data formatting | bytes 262144
Async XLA Ops:
  0.6 1.4 %copy-start.1 = (s32[32,2]{0,1:T(2,128)S(1)}, s32[32,2]{0,1:T(2,128)}, u32[]{:S(2)}) copy-start(s32[32,2]{0,1:T(2,128)} %param.14) | copy-start | bytes 772
  2.0 0.7 %copy-start.2 = (s32[32,2]{0,1:T(2,128)S(1)}, s32[32,2]{0,1:T(2,128)}, u32[]{:S(2)}) copy-start(s32[32,2]{0,1:T(2,128)} %param.15) | copy-start | bytes 772
  54.0 1.6 %copy-start = (bf16[1,4,128,128]{3,2,1,0:T(8,128)(2,1)S(1)}, bf16[1,4,128,128]{3,2,1,0:T(8,128)(2,1)}, u32[]{:S(2)}) copy-start(bf16[1,4,128,128]{3,2,1,0:T(8,128)(2,1)} %get-tuple-element.5) | copy-start | bytes 393220

commit v2 on v1

v2 whole, which is shorter than its diff:
```python
import functools

import jax
import jax.numpy as jnp
from jax import lax
from jax.experimental import pallas as pl
from jax.experimental.pallas import tpu as pltpu
from jax.sharding import PartitionSpec as P

MESH = pl.DeviceIdType.MESH
BLOCK = 128
MARGIN = 2
BAND = 3
F32 = jnp.float32
BF16 = jnp.bfloat16

NN = (((1,), (0,)), ((), ()))
NT = (((1,), (1,)), ((), ()))
TN = (((0,), (0,)), ((), ()))


def dot(a, b, dims=NN):
    return lax.dot_general(a, b, dims, preferred_element_type=F32)


def kernel(
    views,
    slabs,
    feat,
    conv_w,
    q_w,
    k_w,
    v_w,
    partners,
    widths,
    bands,
    grad_att,
    att_out,
    grad_out,
    fbuf,
    wconv,
    wq,
    wk,
    wv,
    dabuf,
    hwin,
    cand,
    wsel,
    qa,
    pd,
    att,
    own,
    gmar,
    rmar,
    ztot,
    zin,
    gout,
    load_sem,
    halo_send,
    halo_recv,
    z_send,
    z_recv,
    m_send,
    m_recv,
    b_send,
    b_recv,
    y_send,
    y_recv,
    out_sem,
):
    step = views // min(16, views)
    rows = dabuf.shape[0]
    width, channels = dabuf.shape[1], dabuf.shape[2]
    reach = MARGIN + 1
    cam = lax.axis_index("cam")
    slab = lax.axis_index("row")
    cam_r, cam_l = lax.rem(cam + step, views), lax.rem(cam + views - step, views)
    odd = lax.rem(slab, 2)

    def by_core(even_value, odd_value):
        return even_value + (odd_value - even_value) * odd

    inner_slab = by_core(slab + 1, slab - 1)
    outer_slab = by_core(lax.rem(slab + slabs - 1, slabs), lax.rem(slab + 1, slabs))
    right, left = (cam_r, slab), (cam_l, slab)
    inner, outer = (cam, inner_slab), (cam, outer_slab)

    barrier = pltpu.get_barrier_semaphore()
    for peer in (outer, inner, right, left):
        pl.semaphore_signal(barrier, inc=1, device_id=peer, device_id_type=MESH)

    loads = [
        pltpu.make_async_copy(feat.at[0], fbuf.at[pl.ds(reach, rows)], load_sem.at[0]),
        pltpu.make_async_copy(conv_w, wconv, load_sem.at[1]),
        pltpu.make_async_copy(grad_att.at[0], dabuf, load_sem.at[2]),
        pltpu.make_async_copy(v_w, wv, load_sem.at[3]),
        pltpu.make_async_copy(q_w, wq, load_sem.at[4]),
        pltpu.make_async_copy(k_w, wk, load_sem.at[5]),
    ]
    for load in loads:
        load.start()

    def remote(src, dst, send, recv, peer):
        return pltpu.make_async_remote_copy(
            src_ref=src, dst_ref=dst, send_sem=send, recv_sem=recv, device_id=peer, device_id_type=MESH
        )

    halo_outer = remote(
        feat.at[0, pl.ds(by_core(0, rows - reach), reach)],
        fbuf.at[pl.ds(by_core(rows + reach, 0), reach)],
        halo_send.at[0],
        halo_recv.at[0],
        outer,
    )
    halo_inner = remote(
        feat.at[0, by_core(rows - 1, 0)],
        fbuf.at[by_core(reach - 1, rows + reach)],
        halo_send.at[1],
        halo_recv.at[1],
        inner,
    )
    edge_row = by_core(MARGIN + rows - 1, MARGIN)
    far_rows = by_core(0, MARGIN + rows - 1)
    places = [*range(MARGIN + 1, MARGIN + rows - 1), edge_row, *[far_rows + k for k in range(reach)]]
    n_inner = rows - 1

    def near(k):
        r = places[k]
        return (
            remote(hwin.at[r], cand.at[0, r], z_send.at[0, k], z_recv.at[0, k], right),
            remote(hwin.at[r], cand.at[2, r], z_send.at[2, k], z_recv.at[2, k], left),
        )

    def far(k):
        r = places[k]
        return (
            remote(cand.at[0, r], cand.at[1, r], z_send.at[1, k], z_recv.at[1, k], right),
            remote(cand.at[2, r], cand.at[3, r], z_send.at[3, k], z_recv.at[3, k], left),
        )

    def conv(start, count):
        total = None
        for dy in range(3):
            weight = jnp.concatenate([wconv[dy, 0], wconv[dy, 1], wconv[dy, 2]], axis=1)
            tap = fbuf[pl.ds(start + dy, count)].reshape(count * width, channels)
            part = dot(tap, weight)
            total = part if total is None else total + part
        size = count * width
        pixel = lax.rem(lax.broadcasted_iota(jnp.int32, (size, channels), 0), width)
        before = pltpu.roll(total[:, :channels], 1, 0)
        after = pltpu.roll(total[:, 2 * channels :], size - 1, 0)
        out = total[:, channels : 2 * channels]
        out = out + jnp.where(pixel == 0, 0.0, before) + jnp.where(pixel == width - 1, 0.0, after)
        hwin[pl.ds(start, count)] = out.astype(BF16).reshape(count, width, channels)

    def relay(ks):
        for k in ks:
            for near_copy, far_copy in zip(near(k), far(k)):
                near_copy.wait_recv()
                far_copy.start()

    def launch(ks):
        for k in ks:
            for copy in near(k):
                copy.start()

    pl.semaphore_wait(barrier, 4)
    halo_outer.start()
    halo_inner.start()
    loads[0].wait()
    loads[1].wait()
    conv(MARGIN + 1, rows - 2)
    launch(range(rows - 2))

    loads[2].wait()
    loads[3].wait()
    loads[4].wait()
    loads[5].wait()
    grad_v = dot(dabuf[...].reshape(rows * width, channels), wv[...], NT).astype(BF16)
    qa[:, pl.ds(width, width), :] = grad_v.reshape(rows, width, channels)
    pd[:, 2 * BAND] = jnp.zeros((rows, BLOCK, 2 * width), BF16)

    halo_inner.wait_recv()
    conv(edge_row, 1)
    launch([rows - 2])
    relay(range(n_inner))

    halo_outer.wait_recv()

    @pl.when(jnp.logical_or(slab == 0, slab == slabs - 1))
    def _():
        fbuf[pl.ds(by_core(0, rows + reach), reach)] = jnp.zeros((reach, width, channels), BF16)

    conv(far_rows, reach)
    launch(range(n_inner, n_inner + reach))

    scale = channels**-0.5
    queries = dot(hwin[pl.ds(MARGIN, rows)].reshape(rows * width, channels), wq[...]).astype(BF16)
    queries = (dot(queries, wk[...], NT) * scale).astype(BF16)
    qa[:, pl.ds(0, width), :] = queries.reshape(rows, width, channels)

    gap0 = lax.rem(cam - partners[0, cam] + views, views)
    gap1 = lax.rem(partners[1, cam] - cam + views, views)

    def select(ks):
        for k in ks:
            r = places[k]
            for copy in far(k):
                copy.wait_recv()
            wsel[0, r] = jnp.where(gap0 == step, cand[0, r], cand[1, r])
            wsel[1, r] = jnp.where(gap1 == step, cand[2, r], cand[3, r])

    relay(range(n_inner, n_inner + reach))
    select(range(n_inner))
    mine = pl.ds(by_core(rows, MARGIN), MARGIN)
    theirs = pl.ds(by_core(0, MARGIN + rows), MARGIN)
    margins = [
        remote(wsel.at[side, mine], wsel.at[side, theirs], m_send.at[side], m_recv.at[side], inner)
        for side in range(2)
    ]
    for copy in margins:
        copy.start()
    select(range(n_inner, n_inner + reach))
    for copy in margins:
        copy.wait_recv()

    base = slab * rows - MARGIN

    def attend(q, carry):
        qa_here = qa[q]
        keys, exps, grads = [], [], []
        total, weighted = None, None
        for side in range(2):
            for slot in range(BAND):
                place = jnp.clip(bands[0, slot, side, q] - base, 0, rows + 2 * MARGIN - 1)
                block = wsel[side, place]
                both = dot(block, qa_here, NT)
                live = jnp.where(slot < widths[side, cam], 1.0, 0.0).astype(F32)
                expo = jnp.where(live > 0.0, jnp.exp(both[:, :width]), 0.0)
                grad = both[:, width:]
                keys.append(block)
                exps.append(expo)
                grads.append(grad)
                here = jnp.sum(expo, axis=0, keepdims=True)
                here_w = jnp.sum(expo * grad, axis=0, keepdims=True)
                total = here if total is None else total + here
                weighted = here_w if weighted is None else weighted + here_w
        inverse = 1.0 / total
        delta = weighted * inverse
        pairs = []
        for place in range(2 * BAND):
            prob = exps[place] * inverse
            score = prob * (grads[place] - delta)
            pair = jnp.concatenate([score.astype(BF16), prob.astype(BF16)], axis=1)
            pd[q, place] = pair
            pairs.append(pair)
        mixed = dot(jnp.concatenate(keys, axis=0), jnp.concatenate(pairs, axis=0), TN).astype(BF16)
        att[q] = dot(mixed[:, width:], wv[...], TN).astype(BF16)
        grad_q = (dot(mixed[:, :width], wk[...], TN) * scale).astype(BF16)
        own[q] = dot(grad_q, wq[...], NT)
        return carry

    lax.fori_loop(0, rows, attend, 0)

    att_copy = pltpu.make_async_copy(att, att_out.at[0], out_sem.at[0])
    att_copy.start()

    def place_of(q, side, row):
        place = jnp.int32(2 * BAND)
        for slot in range(BAND):
            place = jnp.where(bands[0, slot, side, q] - base == row, side * BAND + slot, place)
        return place

    def key_grads(first):
        summed = None
        for q in range(rows):
            lhs = jnp.concatenate(
                [pd[q, place_of(q, side, first + i)] for side in range(2) for i in range(MARGIN)], axis=0
            )
            part = dot(lhs, qa[q])
            summed = part if summed is None else summed + part
        return summed.reshape(2, MARGIN, BLOCK, channels)

    gmar[1] = key_grads(by_core(0, MARGIN + rows)).astype(BF16)
    back = [
        remote(gmar.at[0], rmar.at[0], b_send.at[0], b_recv.at[0], inner),
        remote(gmar.at[1], rmar.at[1], b_send.at[1], b_recv.at[1], outer),
    ]
    back[1].start()
    gmar[0] = key_grads(by_core(MARGIN + rows, 0)).astype(BF16)
    back[0].start()

    def totals(half):
        return (
            remote(ztot.at[0, half], zin.at[0, half], y_send.at[0, half], y_recv.at[0, half], left),
            remote(ztot.at[1, half], zin.at[1, half], y_send.at[1, half], y_recv.at[1, half], right),
        )

    def relays(half):
        return (
            remote(zin.at[0, half], zin.at[2, half], y_send.at[2, half], y_recv.at[2, half], left),
            remote(zin.at[1, half], zin.at[3, half], y_send.at[3, half], y_recv.at[3, half], right),
        )

    firsts = (by_core(MARGIN, 0), by_core(0, MARGIN))

    def send_half(half):
        summed = key_grads(MARGIN + firsts[half])
        back[half].wait_recv()
        ztot[:, half] = (summed + rmar[half].astype(F32)).astype(BF16)
        for copy in totals(half):
            copy.start()

    def relay_half(half):
        for copy, onward in zip(totals(half), relays(half)):
            copy.wait_recv()
            onward.start()

    send_half(0)
    send_half(1)
    relay_half(0)
    relay_half(1)

    def gap_is(other, side, distance):
        other = lax.rem(other + 2 * views, views)
        gap = other - partners[0, other] if side == 0 else partners[1, other] - other
        return jnp.where(lax.rem(gap + views, views) == distance, 1, 0)

    use = (
        gap_is(cam + step, 0, step),
        gap_is(cam - step, 1, step),
        gap_is(cam + 2 * step, 0, 2 * step),
        gap_is(cam - 2 * step, 1, 2 * step),
    )
    for half in range(2):
        for copy in relays(half):
            copy.wait_recv()
        summed = own[pl.ds(firsts[half], MARGIN)]
        for source in range(4):
            summed = summed + jnp.where(use[source] > 0, zin[source, half].astype(F32), 0.0)
        gout[pl.ds(firsts[half], MARGIN)] = summed.astype(BF16)
    grad_copy = pltpu.make_async_copy(gout, grad_out.at[0], out_sem.at[1])
    grad_copy.start()

    halo_outer.wait_send()
    halo_inner.wait_send()
    for k in range(n_inner + reach):
        for copy in (*near(k), *far(k)):
            copy.wait_send()
    for copy in (*margins, *back):
        copy.wait_send()
    for half in range(2):
        for copy in (*totals(half), *relays(half)):
            copy.wait_send()
    att_copy.wait()
    grad_copy.wait()


def local(
    views,
    slabs,
    features_in,
    conv_weight,
    q_weight,
    k_weight,
    v_weight,
    partners,
    band_widths,
    bands,
    grad_attended,
):
    _, rows, width, channels = features_in.shape
    block = (width, channels)
    chunks = rows + MARGIN
    hbm = pl.BlockSpec(memory_space=pl.ANY)
    smem = pl.BlockSpec(memory_space=pltpu.SMEM)
    dma = pltpu.SemaphoreType.DMA
    out = jax.ShapeDtypeStruct(features_in.shape, BF16)
    return pl.pallas_call(
        functools.partial(kernel, views, slabs),
        out_shape=(out, out),
        in_specs=[hbm, hbm, hbm, hbm, hbm, smem, smem, smem, hbm],
        out_specs=(hbm, hbm),
        scratch_shapes=[
            pltpu.VMEM((rows + 2 * MARGIN + 2, *block), BF16),
            pltpu.VMEM(conv_weight.shape, BF16),
            pltpu.VMEM(q_weight.shape, BF16),
            pltpu.VMEM(q_weight.shape, BF16),
            pltpu.VMEM(q_weight.shape, BF16),
            pltpu.VMEM((rows, *block), BF16),
            pltpu.VMEM((rows + 2 * MARGIN, *block), BF16),
            pltpu.VMEM((4, rows + 2 * MARGIN, *block), BF16),
            pltpu.VMEM((2, rows + 2 * MARGIN, *block), BF16),
            pltpu.VMEM((rows, 2 * width, channels), BF16),
            pltpu.VMEM((rows, 2 * BAND + 1, BLOCK, 2 * width), BF16),
            pltpu.VMEM((rows, *block), BF16),
            pltpu.VMEM((rows, *block), F32),
            pltpu.VMEM((2, 2, MARGIN, *block), BF16),
            pltpu.VMEM((2, 2, MARGIN, *block), BF16),
            pltpu.VMEM((2, 2, MARGIN, *block), BF16),
            pltpu.VMEM((4, 2, MARGIN, *block), BF16),
            pltpu.VMEM((rows, *block), BF16),
            dma((6,)),
            dma((2,)),
            dma((2,)),
            dma((4, chunks)),
            dma((4, chunks)),
            dma((2,)),
            dma((2,)),
            dma((2,)),
            dma((2,)),
            dma((4, 2)),
            dma((4, 2)),
            dma((2,)),
        ],
        compiler_params=pltpu.CompilerParams(collective_id=0, has_side_effects=True),
        name="views",
    )(
        features_in,
        conv_weight,
        q_weight,
        k_weight,
        v_weight,
        partners.T,
        band_widths.T,
        bands.transpose(0, 3, 2, 1),
        grad_attended,
    )


def solution(mesh):
    placed = (
        P("cam", "row", None, None),
        P(),
        P(),
        P(),
        P(),
        P(),
        P(),
        P("cam", "row", None, None),
        P("cam", "row", None, None),
    )
    return jax.shard_map(
        functools.partial(local, mesh.shape["cam"], mesh.shape["row"]),
        mesh=mesh,
        in_specs=placed,
        out_specs=(P("cam", "row", None, None), P("cam", "row", None, None)),
        check_vma=False,
    )
```

time: 56.5 us -> 49.7 us (0.88)
  the two profiles are of different devices: /device:TPU:2 before, /device:TPU:32 now
where the time goes in v2:
time: 49.7 us; the launch traced here: 49.6 us
  Pallas kernels  46.6 us (94%)
  local copies, waits for them, and re-layouts  2.26 us (5%)
  between operations  0.65 us (1%)
    pallas_call x1, Pallas kernels, local(): pl.pallas_call(functools.partial(kernel, views, slabs), out_shape=(out, o...  46.6 us
    unnamed x4, local copies, waits for them, and re-layouts  2.26 us

profile of v2, /device:TPU:32, one launch (start us, length us, event | category | flops | bytes accessed | tf_op | source)
XLA Modules:
  0.0 49.6 jit_solution(15131254268232103879)
XLA Ops:
  0.6 46.6 %views.1 = (bf16[1,4,128,128]{3,2,1,0:T(8,128)(2,1)}, bf16[1,4,128,128]{3,2,1,0:T(8,128)(2,1)}) custom-call(bf16[1,4,128,128]{3,2,1,0:T(8,128)(2,1)} %feat.1, bf16[3,3,128,128]{3,2,1,0:T(8,128)(2,1)} %conv_w.1, bf16[128,128]{1,0:T(8,128)(2,1)} %q_w.1, bf16[128,128]{1,0:T(8,128)(2,1)} %k_w.1, bf16[128,128]{1,0:T(8,128)(2,1)} %v_w.1, s32[2,32]{1,0:T(2,128)} %bitcast.4, ...), custom_call_target="tpu_custom_call" | custom-call | tf_op jit(solution)/shard_map/views/pallas_call | solution.py:379
  47.3 0.0 copy-start
  47.3 1.6 %copy.13 = bf16[1,4,128,128]{3,2,1,0:T(8,128)(2,1)} copy(bf16[1,4,128,128]{3,2,1,0:T(8,128)(2,1)} %get-tuple-element.4) | data formatting | bytes 262144
  48.9 0.0 copy-done
  48.9 0.7 %copy.14 = bf16[1,4,128,128]{3,2,1,0:T(8,128)(2,1)} copy(bf16[1,4,128,128]{3,2,1,0:T(8,128)(2,1)S(1)} %copy-done) | data formatting | bytes 262144
Async XLA Ops:
  47.3 1.6 %copy-start = (bf16[1,4,128,128]{3,2,1,0:T(8,128)(2,1)S(1)}, bf16[1,4,128,128]{3,2,1,0:T(8,128)(2,1)}, u32[]{:S(2)}) copy-start(bf16[1,4,128,128]{3,2,1,0:T(8,128)(2,1)} %get-tuple-element.5) | copy-start | bytes 393220

commit v3 on v2

--- a/solution.py
+++ b/solution.py
@@ -48,13 +48,11 @@
     wsel,
     qa,
     pd,
-    att,
     own,
     gmar,
     rmar,
     ztot,
     zin,
-    gout,
     load_sem,
     halo_send,
     halo_recv,
@@ -66,7 +64,6 @@
     b_recv,
     y_send,
     y_recv,
-    out_sem,
 ):
     step = views // min(16, views)
     rows = dabuf.shape[0]
@@ -183,8 +180,7 @@
     halo_inner.wait_recv()
     conv(edge_row, 1)
     launch([rows - 2])
-    relay(range(n_inner))
-
+    relay(range(rows - 2))
     halo_outer.wait_recv()
 
     @pl.when(jnp.logical_or(slab == 0, slab == slabs - 1))
@@ -193,6 +189,7 @@
 
     conv(far_rows, reach)
     launch(range(n_inner, n_inner + reach))
+    relay([rows - 2])
 
     scale = channels**-0.5
     queries = dot(hwin[pl.ds(MARGIN, rows)].reshape(rows * width, channels), wq[...]).astype(BF16)
@@ -226,44 +223,42 @@
 
     base = slab * rows - MARGIN
 
-    def attend(q, carry):
+    def key_block(q, side, slot):
+        return wsel[side, jnp.clip(bands[0, slot, side, q] - base, 0, rows + 2 * MARGIN - 1)]
+
+    lists = [(side, slot) for side in range(2) for slot in range(BAND)]
+
+    def attend(q):
         qa_here = qa[q]
-        keys, exps, grads = [], [], []
+        exps, grads = [], []
         total, weighted = None, None
-        for side in range(2):
-            for slot in range(BAND):
-                place = jnp.clip(bands[0, slot, side, q] - base, 0, rows + 2 * MARGIN - 1)
-                block = wsel[side, place]
-                both = dot(block, qa_here, NT)
-                live = jnp.where(slot < widths[side, cam], 1.0, 0.0).astype(F32)
-                expo = jnp.where(live > 0.0, jnp.exp(both[:, :width]), 0.0)
-                grad = both[:, width:]
-                keys.append(block)
-                exps.append(expo)
-                grads.append(grad)
-                here = jnp.sum(expo, axis=0, keepdims=True)
-                here_w = jnp.sum(expo * grad, axis=0, keepdims=True)
-                total = here if total is None else total + here
-                weighted = here_w if weighted is None else weighted + here_w
+        for side, slot in lists:
+            both = dot(key_block(q, side, slot), qa_here, NT)
+            expo = jnp.where(slot < widths[side, cam], jnp.exp(both[:, :width]), 0.0)
+            grad = both[:, width:]
+            exps.append(expo)
+            grads.append(grad)
+            here = jnp.sum(expo, axis=0, keepdims=True)
+            here_w = jnp.sum(expo * grad, axis=0, keepdims=True)
+            total = here if total is None else total + here
+            weighted = here_w if weighted is None else weighted + here_w
         inverse = 1.0 / total
         delta = weighted * inverse
-        pairs = []
         for place in range(2 * BAND):
             prob = exps[place] * inverse
             score = prob * (grads[place] - delta)
-            pair = jnp.concatenate([score.astype(BF16), prob.astype(BF16)], axis=1)
-            pd[q, place] = pair
-            pairs.append(pair)
-        mixed = dot(jnp.concatenate(keys, axis=0), jnp.concatenate(pairs, axis=0), TN).astype(BF16)
-        att[q] = dot(mixed[:, width:], wv[...], TN).astype(BF16)
+            pd[q, place] = jnp.concatenate([score.astype(BF16), prob.astype(BF16)], axis=1)
+
+    def combine(q):
+        keys = jnp.concatenate([key_block(q, side, slot) for side, slot in lists], axis=0)
+        pairs = pd[q, pl.ds(0, 2 * BAND)].reshape(2 * BAND * BLOCK, 2 * width)
+        mixed = dot(keys, pairs, TN).astype(BF16)
+        att_out[0, q] = dot(mixed[:, width:], wv[...], TN).astype(BF16)
         grad_q = (dot(mixed[:, :width], wk[...], TN) * scale).astype(BF16)
         own[q] = dot(grad_q, wq[...], NT)
-        return carry
-
-    lax.fori_loop(0, rows, attend, 0)
-
-    att_copy = pltpu.make_async_copy(att, att_out.at[0], out_sem.at[0])
-    att_copy.start()
+
+    for q in range(rows):
+        attend(q)
 
     def place_of(q, side, row):
         place = jnp.int32(2 * BAND)
@@ -290,34 +285,41 @@
     gmar[0] = key_grads(by_core(MARGIN + rows, 0)).astype(BF16)
     back[0].start()
 
-    def totals(half):
+    def totals(half, i):
+        k = half * MARGIN + i
         return (
-            remote(ztot.at[0, half], zin.at[0, half], y_send.at[0, half], y_recv.at[0, half], left),
-            remote(ztot.at[1, half], zin.at[1, half], y_send.at[1, half], y_recv.at[1, half], right),
+            remote(ztot.at[0, k], zin.at[0, k], y_send.at[0, k], y_recv.at[0, k], left),
+            remote(ztot.at[1, k], zin.at[1, k], y_send.at[1, k], y_recv.at[1, k], right),
         )
 
-    def relays(half):
+    def relays(half, i):
+        k = half * MARGIN + i
         return (
-            remote(zin.at[0, half], zin.at[2, half], y_send.at[2, half], y_recv.at[2, half], left),
-            remote(zin.at[1, half], zin.at[3, half], y_send.at[3, half], y_recv.at[3, half], right),
+            remote(zin.at[0, k], zin.at[2, k], y_send.at[2, k], y_recv.at[2, k], left),
+            remote(zin.at[1, k], zin.at[3, k], y_send.at[3, k], y_recv.at[3, k], right),
         )
 
     firsts = (by_core(MARGIN, 0), by_core(0, MARGIN))
 
-    def send_half(half):
-        summed = key_grads(MARGIN + firsts[half])
+    def send_half(half, summed):
         back[half].wait_recv()
-        ztot[:, half] = (summed + rmar[half].astype(F32)).astype(BF16)
-        for copy in totals(half):
-            copy.start()
+        for i in range(MARGIN):
+            for side in range(2):
+                ztot[side, half * MARGIN + i] = (summed[side, i] + rmar[half, side, i].astype(F32)).astype(BF16)
+            for copy in totals(half, i):
+                copy.start()
 
     def relay_half(half):
-        for copy, onward in zip(totals(half), relays(half)):
-            copy.wait_recv()
-            onward.start()
-
-    send_half(0)
-    send_half(1)
+        for i in range(MARGIN):
+            for copy, onward in zip(totals(half, i), relays(half, i)):
+                copy.wait_recv()
+                onward.start()
+
+    send_half(0, key_grads(MARGIN + firsts[0]))
+    last_half = key_grads(MARGIN + firsts[1])
+    for q in range(rows):
+        combine(q)
+    send_half(1, last_half)
     relay_half(0)
     relay_half(1)
 
@@ -333,14 +335,13 @@
         gap_is(cam - 2 * step, 1, 2 * step),
     )
     for half in range(2):
-        for copy in relays(half):
-            copy.wait_recv()
-        summed = own[pl.ds(firsts[half], MARGIN)]
-        for source in range(4):
-            summed = summed + jnp.where(use[source] > 0, zin[source, half].astype(F32), 0.0)
-        gout[pl.ds(firsts[half], MARGIN)] = summed.astype(BF16)
-    grad_copy = pltpu.make_async_copy(gout, grad_out.at[0], out_sem.at[1])
-    grad_copy.start()
+        for i in range(MARGIN):
+            for copy in relays(half, i):
+                copy.wait_recv()
+            summed = own[firsts[half] + i]
+            for source in range(4):
+                summed = summed + jnp.where(use[source] > 0, zin[source, half * MARGIN + i].astype(F32), 0.0)
+            grad_out[0, firsts[half] + i] = summed.astype(BF16)
 
     halo_outer.wait_send()
     halo_inner.wait_send()
@@ -350,10 +351,9 @@
     for copy in (*margins, *back):
         copy.wait_send()
     for half in range(2):
-        for copy in (*totals(half), *relays(half)):
-            copy.wait_send()
-    att_copy.wait()
-    grad_copy.wait()
+        for i in range(MARGIN):
+            for copy in (*totals(half, i), *relays(half, i)):
+                copy.wait_send()
 
 
 def local(
@@ -373,6 +373,7 @@
     block = (width, channels)
     chunks = rows + MARGIN
     hbm = pl.BlockSpec(memory_space=pl.ANY)
+    vmem = pl.BlockSpec(memory_space=pltpu.VMEM)
     smem = pl.BlockSpec(memory_space=pltpu.SMEM)
     dma = pltpu.SemaphoreType.DMA
     out = jax.ShapeDtypeStruct(features_in.shape, BF16)
@@ -380,7 +381,7 @@
         functools.partial(kernel, views, slabs),
         out_shape=(out, out),
         in_specs=[hbm, hbm, hbm, hbm, hbm, smem, smem, smem, hbm],
-        out_specs=(hbm, hbm),
+        out_specs=(vmem, vmem),
         scratch_shapes=[
             pltpu.VMEM((rows + 2 * MARGIN + 2, *block), BF16),
             pltpu.VMEM(conv_weight.shape, BF16),
@@ -393,13 +394,11 @@
             pltpu.VMEM((2, rows + 2 * MARGIN, *block), BF16),
             pltpu.VMEM((rows, 2 * width, channels), BF16),
             pltpu.VMEM((rows, 2 * BAND + 1, BLOCK, 2 * width), BF16),
-            pltpu.VMEM((rows, *block), BF16),
             pltpu.VMEM((rows, *block), F32),
             pltpu.VMEM((2, 2, MARGIN, *block), BF16),
             pltpu.VMEM((2, 2, MARGIN, *block), BF16),
-            pltpu.VMEM((2, 2, MARGIN, *block), BF16),
-            pltpu.VMEM((4, 2, MARGIN, *block), BF16),
-            pltpu.VMEM((rows, *block), BF16),
+            pltpu.VMEM((2, rows, *block), BF16),
+            pltpu.VMEM((4, rows, *block), BF16),
             dma((6,)),
             dma((2,)),
             dma((2,)),
@@ -409,9 +408,8 @@
             dma((2,)),
             dma((2,)),
             dma((2,)),
-            dma((4, 2)),
-            dma((4, 2)),
-            dma((2,)),
+            dma((4, rows)),
+            dma((4, rows)),
         ],
         compiler_params=pltpu.CompilerParams(collective_id=0, has_side_effects=True),
         name="views",

time: 49.7 us -> 46 us (0.926)
  the two profiles are of different devices: /device:TPU:32 before, /device:TPU:2 now
where the time goes in v3:
time: 46 us; the launch traced here: 45.7 us
  Pallas kernels  42.8 us (93%)
  local copies, waits for them, and re-layouts  2.26 us (5%)
  between operations  0.65 us (1%)
    pallas_call x1, Pallas kernels, local(): pl.pallas_call(functools.partial(kernel, views, slabs), out_shape=(out, o...  42.8 us
    unnamed x4, local copies, waits for them, and re-layouts  2.26 us

profile of v3, /device:TPU:2, one launch (start us, length us, event | category | flops | bytes accessed | tf_op | source)
XLA Modules:
  0.0 45.7 jit_solution(10683266587821582569)
XLA Ops:
  0.6 42.8 %views.1 = (bf16[1,4,128,128]{3,2,1,0:T(8,128)(2,1)}, bf16[1,4,128,128]{3,2,1,0:T(8,128)(2,1)}) custom-call(bf16[1,4,128,128]{3,2,1,0:T(8,128)(2,1)} %feat.1, bf16[3,3,128,128]{3,2,1,0:T(8,128)(2,1)} %conv_w.1, bf16[128,128]{1,0:T(8,128)(2,1)} %q_w.1, bf16[128,128]{1,0:T(8,128)(2,1)} %k_w.1, bf16[128,128]{1,0:T(8,128)(2,1)} %v_w.1, s32[2,32]{1,0:T(2,128)} %bitcast.4, ...), custom_call_target="tpu_custom_call" | custom-call | tf_op jit(solution)/shard_map/views/pallas_call | solution.py:380
  43.5 0.0 copy-start
  43.5 1.6 %copy.13 = bf16[1,4,128,128]{3,2,1,0:T(8,128)(2,1)} copy(bf16[1,4,128,128]{3,2,1,0:T(8,128)(2,1)} %get-tuple-element.4) | data formatting | bytes 262144
  45.1 0.0 copy-done
  45.1 0.7 %copy.14 = bf16[1,4,128,128]{3,2,1,0:T(8,128)(2,1)} copy(bf16[1,4,128,128]{3,2,1,0:T(8,128)(2,1)S(1)} %copy-done) | data formatting | bytes 262144
Async XLA Ops:
  43.5 1.6 %copy-start = (bf16[1,4,128,128]{3,2,1,0:T(8,128)(2,1)S(1)}, bf16[1,4,128,128]{3,2,1,0:T(8,128)(2,1)}, u32[]{:S(2)}) copy-start(bf16[1,4,128,128]{3,2,1,0:T(8,128)(2,1)} %get-tuple-element.5) | copy-start | bytes 393220

commit v4 on v3

--- a/solution.py
+++ b/solution.py
@@ -31,12 +31,15 @@
     q_w,
     k_w,
     v_w,
+    partners_in,
+    widths_in,
+    bands_in,
+    grad_att,
+    att_out,
+    grad_out,
     partners,
     widths,
     bands,
-    grad_att,
-    att_out,
-    grad_out,
     fbuf,
     wconv,
     wq,
@@ -53,6 +56,8 @@
     rmar,
     ztot,
     zin,
+    att,
+    gout,
     load_sem,
     halo_send,
     halo_recv,
@@ -64,6 +69,7 @@
     b_recv,
     y_send,
     y_recv,
+    out_sem,
 ):
     step = views // min(16, views)
     rows = dabuf.shape[0]
@@ -93,6 +99,9 @@
         pltpu.make_async_copy(v_w, wv, load_sem.at[3]),
         pltpu.make_async_copy(q_w, wq, load_sem.at[4]),
         pltpu.make_async_copy(k_w, wk, load_sem.at[5]),
+        pltpu.make_async_copy(partners_in, partners, load_sem.at[6]),
+        pltpu.make_async_copy(widths_in, widths, load_sem.at[7]),
+        pltpu.make_async_copy(bands_in, bands, load_sem.at[8]),
     ]
     for load in loads:
         load.start()
@@ -102,13 +111,22 @@
             src_ref=src, dst_ref=dst, send_sem=send, recv_sem=recv, device_id=peer, device_id_type=MESH
         )
 
-    halo_outer = remote(
-        feat.at[0, pl.ds(by_core(0, rows - reach), reach)],
-        fbuf.at[pl.ds(by_core(rows + reach, 0), reach)],
-        halo_send.at[0],
-        halo_recv.at[0],
-        outer,
-    )
+    halo_outer = [
+        remote(
+            feat.at[0, by_core(0, rows - 1)],
+            fbuf.at[by_core(rows + reach, reach - 1)],
+            halo_send.at[0],
+            halo_recv.at[0],
+            outer,
+        ),
+        remote(
+            feat.at[0, pl.ds(by_core(1, rows - reach), MARGIN)],
+            fbuf.at[pl.ds(by_core(rows + reach + 1, 0), MARGIN)],
+            halo_send.at[2],
+            halo_recv.at[2],
+            outer,
+        ),
+    ]
     halo_inner = remote(
         feat.at[0, by_core(rows - 1, 0)],
         fbuf.at[by_core(reach - 1, rows + reach)],
@@ -117,8 +135,9 @@
         inner,
     )
     edge_row = by_core(MARGIN + rows - 1, MARGIN)
-    far_rows = by_core(0, MARGIN + rows - 1)
-    places = [*range(MARGIN + 1, MARGIN + rows - 1), edge_row, *[far_rows + k for k in range(reach)]]
+    outer_row = by_core(MARGIN, MARGIN + rows - 1)
+    far_rows = by_core(0, MARGIN + rows)
+    places = [*range(MARGIN + 1, MARGIN + rows - 1), edge_row, outer_row, *[far_rows + k for k in range(MARGIN)]]
     n_inner = rows - 1
 
     def near(k):
@@ -161,12 +180,13 @@
             for copy in near(k):
                 copy.start()
 
-    pl.semaphore_wait(barrier, 4)
-    halo_outer.start()
-    halo_inner.start()
     loads[0].wait()
     loads[1].wait()
     conv(MARGIN + 1, rows - 2)
+    pl.semaphore_wait(barrier, 4)
+    halo_outer[0].start()
+    halo_inner.start()
+    halo_outer[1].start()
     launch(range(rows - 2))
 
     loads[2].wait()
@@ -180,22 +200,27 @@
     halo_inner.wait_recv()
     conv(edge_row, 1)
     launch([rows - 2])
-    relay(range(rows - 2))
-    halo_outer.wait_recv()
+    relay([0])
+    halo_outer[0].wait_recv()
 
     @pl.when(jnp.logical_or(slab == 0, slab == slabs - 1))
     def _():
-        fbuf[pl.ds(by_core(0, rows + reach), reach)] = jnp.zeros((reach, width, channels), BF16)
-
-    conv(far_rows, reach)
-    launch(range(n_inner, n_inner + reach))
-    relay([rows - 2])
+        fbuf[by_core(reach - 1, rows + reach)] = jnp.zeros((width, channels), BF16)
+
+    conv(outer_row, 1)
+    launch([n_inner])
+    halo_outer[1].wait_recv()
+    conv(far_rows, MARGIN)
+    launch(range(n_inner + 1, n_inner + reach))
+    relay(range(1, n_inner))
 
     scale = channels**-0.5
     queries = dot(hwin[pl.ds(MARGIN, rows)].reshape(rows * width, channels), wq[...]).astype(BF16)
     queries = (dot(queries, wk[...], NT) * scale).astype(BF16)
     qa[:, pl.ds(0, width), :] = queries.reshape(rows, width, channels)
 
+    for load in loads[6:]:
+        load.wait()
     gap0 = lax.rem(cam - partners[0, cam] + views, views)
     gap1 = lax.rem(partners[1, cam] - cam + views, views)
 
@@ -249,11 +274,14 @@
             score = prob * (grads[place] - delta)
             pd[q, place] = jnp.concatenate([score.astype(BF16), prob.astype(BF16)], axis=1)
 
+    att_copies = [pltpu.make_async_copy(att.at[q], att_out.at[0, q], out_sem.at[q]) for q in range(rows)]
+
     def combine(q):
         keys = jnp.concatenate([key_block(q, side, slot) for side, slot in lists], axis=0)
         pairs = pd[q, pl.ds(0, 2 * BAND)].reshape(2 * BAND * BLOCK, 2 * width)
         mixed = dot(keys, pairs, TN).astype(BF16)
-        att_out[0, q] = dot(mixed[:, width:], wv[...], TN).astype(BF16)
+        att[q] = dot(mixed[:, width:], wv[...], TN).astype(BF16)
+        att_copies[q].start()
         grad_q = (dot(mixed[:, :width], wk[...], TN) * scale).astype(BF16)
         own[q] = dot(grad_q, wq[...], NT)
 
@@ -266,24 +294,25 @@
             place = jnp.where(bands[0, slot, side, q] - base == row, side * BAND + slot, place)
         return place
 
-    def key_grads(first):
+    def key_grads(first, count):
         summed = None
         for q in range(rows):
             lhs = jnp.concatenate(
-                [pd[q, place_of(q, side, first + i)] for side in range(2) for i in range(MARGIN)], axis=0
+                [pd[q, place_of(q, side, first + i)] for i in range(count) for side in range(2)], axis=0
             )
             part = dot(lhs, qa[q])
             summed = part if summed is None else summed + part
-        return summed.reshape(2, MARGIN, BLOCK, channels)
-
-    gmar[1] = key_grads(by_core(0, MARGIN + rows)).astype(BF16)
+        return summed.reshape(count, 2, BLOCK, channels)
+
     back = [
-        remote(gmar.at[0], rmar.at[0], b_send.at[0], b_recv.at[0], inner),
-        remote(gmar.at[1], rmar.at[1], b_send.at[1], b_recv.at[1], outer),
+        [remote(gmar.at[0], rmar.at[0], b_send.at[0], b_recv.at[0], inner)],
+        [remote(gmar.at[1, i], rmar.at[1, i], b_send.at[1 + i], b_recv.at[1 + i], outer) for i in range(MARGIN)],
     ]
-    back[1].start()
-    gmar[0] = key_grads(by_core(MARGIN + rows, 0)).astype(BF16)
-    back[0].start()
+    for i in range(MARGIN):
+        gmar[1, i] = key_grads(by_core(0, MARGIN + rows) + i, 1)[0].astype(BF16)
+        back[1][i].start()
+    gmar[0] = key_grads(by_core(MARGIN + rows, 0), MARGIN).astype(BF16)
+    back[0][0].start()
 
     def totals(half, i):
         k = half * MARGIN + i
@@ -301,13 +330,11 @@
 
     firsts = (by_core(MARGIN, 0), by_core(0, MARGIN))
 
-    def send_half(half, summed):
-        back[half].wait_recv()
-        for i in range(MARGIN):
-            for side in range(2):
-                ztot[side, half * MARGIN + i] = (summed[side, i] + rmar[half, side, i].astype(F32)).astype(BF16)
-            for copy in totals(half, i):
-                copy.start()
+    def send_row(half, i, summed):
+        k = half * MARGIN + i
+        ztot[:, k] = (summed[i] + rmar[half, i].astype(F32)).astype(BF16)
+        for copy in totals(half, i):
+            copy.start()
 
     def relay_half(half):
         for i in range(MARGIN):
@@ -315,12 +342,21 @@
                 copy.wait_recv()
                 onward.start()
 
-    send_half(0, key_grads(MARGIN + firsts[0]))
-    last_half = key_grads(MARGIN + firsts[1])
-    for q in range(rows):
+    first_half = key_grads(MARGIN + firsts[0], MARGIN)
+    back[0][0].wait_recv()
+    for i in range(MARGIN):
+        send_row(0, i, first_half)
+    last_half = key_grads(MARGIN + firsts[1], MARGIN)
+    for q in range(rows // 2):
         combine(q)
-    send_half(1, last_half)
+    back[1][0].wait_recv()
+    send_row(1, 0, last_half)
+    combine(rows // 2)
+    back[1][1].wait_recv()
+    send_row(1, 1, last_half)
     relay_half(0)
+    for q in range(rows // 2 + 1, rows):
+        combine(q)
     relay_half(1)
 
     def gap_is(other, side, distance):
@@ -334,6 +370,13 @@
         gap_is(cam + 2 * step, 0, 2 * step),
         gap_is(cam - 2 * step, 1, 2 * step),
     )
+    grad_copies = [
+        pltpu.make_async_copy(
+            gout.at[half, i], grad_out.at[0, firsts[half] + i], out_sem.at[rows + half * MARGIN + i]
+        )
+        for half in range(2)
+        for i in range(MARGIN)
+    ]
     for half in range(2):
         for i in range(MARGIN):
             for copy in relays(half, i):
@@ -341,19 +384,23 @@
             summed = own[firsts[half] + i]
             for source in range(4):
                 summed = summed + jnp.where(use[source] > 0, zin[source, half * MARGIN + i].astype(F32), 0.0)
-            grad_out[0, firsts[half] + i] = summed.astype(BF16)
-
-    halo_outer.wait_send()
+            gout[half, i] = summed.astype(BF16)
+            grad_copies[half * MARGIN + i].start()
+
+    for copy in halo_outer:
+        copy.wait_send()
     halo_inner.wait_send()
     for k in range(n_inner + reach):
         for copy in (*near(k), *far(k)):
             copy.wait_send()
-    for copy in (*margins, *back):
+    for copy in (*margins, *back[0], *back[1]):
         copy.wait_send()
     for half in range(2):
         for i in range(MARGIN):
             for copy in (*totals(half, i), *relays(half, i)):
                 copy.wait_send()
+    for copy in (*att_copies, *grad_copies):
+        copy.wait()
 
 
 def local(
@@ -373,16 +420,17 @@
     block = (width, channels)
     chunks = rows + MARGIN
     hbm = pl.BlockSpec(memory_space=pl.ANY)
-    vmem = pl.BlockSpec(memory_space=pltpu.VMEM)
-    smem = pl.BlockSpec(memory_space=pltpu.SMEM)
     dma = pltpu.SemaphoreType.DMA
     out = jax.ShapeDtypeStruct(features_in.shape, BF16)
     return pl.pallas_call(
         functools.partial(kernel, views, slabs),
         out_shape=(out, out),
-        in_specs=[hbm, hbm, hbm, hbm, hbm, smem, smem, smem, hbm],
-        out_specs=(vmem, vmem),
+        in_specs=[hbm] * 9,
+        out_specs=(hbm, hbm),
         scratch_shapes=[
+            pltpu.SMEM(partners.shape[::-1], jnp.int32),
+            pltpu.SMEM(band_widths.shape[::-1], jnp.int32),
+            pltpu.SMEM((1, *bands.shape[:0:-1]), jnp.int32),
             pltpu.VMEM((rows + 2 * MARGIN + 2, *block), BF16),
             pltpu.VMEM(conv_weight.shape, BF16),
             pltpu.VMEM(q_weight.shape, BF16),
@@ -399,17 +447,20 @@
             pltpu.VMEM((2, 2, MARGIN, *block), BF16),
             pltpu.VMEM((2, rows, *block), BF16),
             pltpu.VMEM((4, rows, *block), BF16),
-            dma((6,)),
-            dma((2,)),
-            dma((2,)),
+            pltpu.VMEM((rows, *block), BF16),
+            pltpu.VMEM((2, MARGIN, *block), BF16),
+            dma((9,)),
+            dma((3,)),
+            dma((3,)),
             dma((4, chunks)),
             dma((4, chunks)),
             dma((2,)),
             dma((2,)),
-            dma((2,)),
-            dma((2,)),
+            dma((1 + MARGIN,)),
+            dma((1 + MARGIN,)),
             dma((4, rows)),
             dma((4, rows)),
+            dma((2 * rows,)),
         ],
         compiler_params=pltpu.CompilerParams(collective_id=0, has_side_effects=True),
         name="views",

time: 46 us -> 44.4 us (0.965)
  Pallas kernels: 42.8 us -> 41.3 us
    pallas_call x1, Pallas kernels: 42.8 us -> 41.3 us  [local(): pl.pallas_call(functools.partial(kernel, views, slabs), out_shape=(out, o...]
where the time goes in v4:
time: 44.4 us; the launch traced here: 44.2 us
  Pallas kernels  41.3 us (93%)
  local copies, waits for them, and re-layouts  2.26 us (5%)
  between operations  0.65 us (1%)
    pallas_call x1, Pallas kernels, local(): pl.pallas_call(functools.partial(kernel, views, slabs), out_shape=(out, o...  41.3 us
    unnamed x4, local copies, waits for them, and re-layouts  2.26 us

profile of v4, /device:TPU:2, one launch (start us, length us, event | category | flops | bytes accessed | tf_op | source)
XLA Modules:
  0.0 44.2 jit_solution(886041445445608506)
XLA Ops:
  0.6 41.3 %views.1 = (bf16[1,4,128,128]{3,2,1,0:T(8,128)(2,1)}, bf16[1,4,128,128]{3,2,1,0:T(8,128)(2,1)}) custom-call(bf16[1,4,128,128]{3,2,1,0:T(8,128)(2,1)} %feat.1, bf16[3,3,128,128]{3,2,1,0:T(8,128)(2,1)} %conv_w.1, bf16[128,128]{1,0:T(8,128)(2,1)} %q_w.1, bf16[128,128]{1,0:T(8,128)(2,1)} %k_w.1, bf16[128,128]{1,0:T(8,128)(2,1)} %v_w.1, s32[2,32]{1,0:T(2,128)} %bitcast.4, ...), custom_call_target="tpu_custom_call" | custom-call | tf_op jit(solution)/shard_map/views/pallas_call | solution.py:425
  42.0 0.0 copy-start
  42.0 1.6 %copy.13 = bf16[1,4,128,128]{3,2,1,0:T(8,128)(2,1)} copy(bf16[1,4,128,128]{3,2,1,0:T(8,128)(2,1)} %get-tuple-element.4) | data formatting | bytes 262144
  43.6 0.0 copy-done
  43.6 0.7 %copy.14 = bf16[1,4,128,128]{3,2,1,0:T(8,128)(2,1)} copy(bf16[1,4,128,128]{3,2,1,0:T(8,128)(2,1)S(1)} %copy-done) | data formatting | bytes 262144
Async XLA Ops:
  42.0 1.6 %copy-start = (bf16[1,4,128,128]{3,2,1,0:T(8,128)(2,1)S(1)}, bf16[1,4,128,128]{3,2,1,0:T(8,128)(2,1)}, u32[]{:S(2)}) copy-start(bf16[1,4,128,128]{3,2,1,0:T(8,128)(2,1)} %get-tuple-element.5) | copy-start | bytes 393220

commit v5 on v4

--- a/solution.py
+++ b/solution.py
@@ -35,8 +35,7 @@
     widths_in,
     bands_in,
     grad_att,
-    att_out,
-    grad_out,
+    both_out,
     partners,
     widths,
     bands,
@@ -56,8 +55,6 @@
     rmar,
     ztot,
     zin,
-    att,
-    gout,
     load_sem,
     halo_send,
     halo_recv,
@@ -69,7 +66,6 @@
     b_recv,
     y_send,
     y_recv,
-    out_sem,
 ):
     step = views // min(16, views)
     rows = dabuf.shape[0]
@@ -143,15 +139,15 @@
     def near(k):
         r = places[k]
         return (
-            remote(hwin.at[r], cand.at[0, r], z_send.at[0, k], z_recv.at[0, k], right),
-            remote(hwin.at[r], cand.at[2, r], z_send.at[2, k], z_recv.at[2, k], left),
+            remote(hwin.at[r], cand.at[0, r], z_send, z_recv.at[0, k], right),
+            remote(hwin.at[r], cand.at[2, r], z_send, z_recv.at[2, k], left),
         )
 
     def far(k):
         r = places[k]
         return (
-            remote(cand.at[0, r], cand.at[1, r], z_send.at[1, k], z_recv.at[1, k], right),
-            remote(cand.at[2, r], cand.at[3, r], z_send.at[3, k], z_recv.at[3, k], left),
+            remote(cand.at[0, r], cand.at[1, r], z_send, z_recv.at[1, k], right),
+            remote(cand.at[2, r], cand.at[3, r], z_send, z_recv.at[3, k], left),
         )
 
     def conv(start, count):
@@ -274,14 +270,11 @@
             score = prob * (grads[place] - delta)
             pd[q, place] = jnp.concatenate([score.astype(BF16), prob.astype(BF16)], axis=1)
 
-    att_copies = [pltpu.make_async_copy(att.at[q], att_out.at[0, q], out_sem.at[q]) for q in range(rows)]
-
     def combine(q):
         keys = jnp.concatenate([key_block(q, side, slot) for side, slot in lists], axis=0)
         pairs = pd[q, pl.ds(0, 2 * BAND)].reshape(2 * BAND * BLOCK, 2 * width)
         mixed = dot(keys, pairs, TN).astype(BF16)
-        att[q] = dot(mixed[:, width:], wv[...], TN).astype(BF16)
-        att_copies[q].start()
+        both_out[0, q] = dot(mixed[:, width:], wv[...], TN).astype(BF16)
         grad_q = (dot(mixed[:, :width], wk[...], TN) * scale).astype(BF16)
         own[q] = dot(grad_q, wq[...], NT)
 
@@ -317,15 +310,15 @@
     def totals(half, i):
         k = half * MARGIN + i
         return (
-            remote(ztot.at[0, k], zin.at[0, k], y_send.at[0, k], y_recv.at[0, k], left),
-            remote(ztot.at[1, k], zin.at[1, k], y_send.at[1, k], y_recv.at[1, k], right),
+            remote(ztot.at[0, k], zin.at[0, k], y_send, y_recv.at[0, k], left),
+            remote(ztot.at[1, k], zin.at[1, k], y_send, y_recv.at[1, k], right),
         )
 
     def relays(half, i):
         k = half * MARGIN + i
         return (
-            remote(zin.at[0, k], zin.at[2, k], y_send.at[2, k], y_recv.at[2, k], left),
-            remote(zin.at[1, k], zin.at[3, k], y_send.at[3, k], y_recv.at[3, k], right),
+            remote(zin.at[0, k], zin.at[2, k], y_send, y_recv.at[2, k], left),
+            remote(zin.at[1, k], zin.at[3, k], y_send, y_recv.at[3, k], right),
         )
 
     firsts = (by_core(MARGIN, 0), by_core(0, MARGIN))
@@ -370,13 +363,6 @@
         gap_is(cam + 2 * step, 0, 2 * step),
         gap_is(cam - 2 * step, 1, 2 * step),
     )
-    grad_copies = [
-        pltpu.make_async_copy(
-            gout.at[half, i], grad_out.at[0, firsts[half] + i], out_sem.at[rows + half * MARGIN + i]
-        )
-        for half in range(2)
-        for i in range(MARGIN)
-    ]
     for half in range(2):
         for i in range(MARGIN):
             for copy in relays(half, i):
@@ -384,23 +370,16 @@
             summed = own[firsts[half] + i]
             for source in range(4):
                 summed = summed + jnp.where(use[source] > 0, zin[source, half * MARGIN + i].astype(F32), 0.0)
-            gout[half, i] = summed.astype(BF16)
-            grad_copies[half * MARGIN + i].start()
+            both_out[1, firsts[half] + i] = summed.astype(BF16)
 
     for copy in halo_outer:
         copy.wait_send()
     halo_inner.wait_send()
-    for k in range(n_inner + reach):
-        for copy in (*near(k), *far(k)):
-            copy.wait_send()
+    sent = cand.at[:, pl.ds(0, n_inner + reach)]
+    pltpu.make_async_copy(sent, sent, z_send).wait()
     for copy in (*margins, *back[0], *back[1]):
         copy.wait_send()
-    for half in range(2):
-        for i in range(MARGIN):
-            for copy in (*totals(half, i), *relays(half, i)):
-                copy.wait_send()
-    for copy in (*att_copies, *grad_copies):
-        copy.wait()
+    pltpu.make_async_copy(zin, zin, y_send).wait()
 
 
 def local(
@@ -421,12 +400,12 @@
     chunks = rows + MARGIN
     hbm = pl.BlockSpec(memory_space=pl.ANY)
     dma = pltpu.SemaphoreType.DMA
-    out = jax.ShapeDtypeStruct(features_in.shape, BF16)
-    return pl.pallas_call(
+    out = jax.ShapeDtypeStruct((2, *features_in.shape[1:]), BF16)
+    both = pl.pallas_call(
         functools.partial(kernel, views, slabs),
-        out_shape=(out, out),
+        out_shape=out,
         in_specs=[hbm] * 9,
-        out_specs=(hbm, hbm),
+        out_specs=pl.BlockSpec(memory_space=pltpu.VMEM),
         scratch_shapes=[
             pltpu.SMEM(partners.shape[::-1], jnp.int32),
             pltpu.SMEM(band_widths.shape[::-1], jnp.int32),
@@ -447,34 +426,37 @@
             pltpu.VMEM((2, 2, MARGIN, *block), BF16),
             pltpu.VMEM((2, rows, *block), BF16),
             pltpu.VMEM((4, rows, *block), BF16),
-            pltpu.VMEM((rows, *block), BF16),
-            pltpu.VMEM((2, MARGIN, *block), BF16),
             dma((9,)),
             dma((3,)),
             dma((3,)),
-            dma((4, chunks)),
+            dma,
             dma((4, chunks)),
             dma((2,)),
             dma((2,)),
             dma((1 + MARGIN,)),
             dma((1 + MARGIN,)),
+            dma,
             dma((4, rows)),
-            dma((4, rows)),
-            dma((2 * rows,)),
         ],
-        compiler_params=pltpu.CompilerParams(collective_id=0, has_side_effects=True),
+        compiler_params=pltpu.CompilerParams(collective_id=0, has_side_effects=True, vmem_limit_bytes=32 << 20),
         name="views",
     )(
-        features_in,
-        conv_weight,
-        q_weight,
-        k_weight,
-        v_weight,
-        partners.T,
-        band_widths.T,
-        bands.transpose(0, 3, 2, 1),
-        grad_attended,
+        *[
+            pltpu.with_memory_space_constraint(array, pltpu.HBM)
+            for array in (
+                features_in,
+                conv_weight,
+                q_weight,
+                k_weight,
+                v_weight,
+                partners.T,
+                band_widths.T,
+                bands.transpose(0, 3, 2, 1),
+                grad_attended,
+            )
+        ]
     )
+    return both[:1], both[1:]
 
 
 def solution(mesh):

time: 44.4 us -> 41.8 us (0.941)
  local copies, waits for them, and re-layouts: 2.26 us -> 0.72 us
  Pallas kernels: 41.3 us -> 40.3 us
    unnamed x4 -> x0, local copies, waits for them, and re-layouts: 2.26 us -> none
    pallas_call x1, Pallas kernels: 41.3 us -> 40.3 us  [local(): pl.pallas_call(functools.partial(kernel, views, slabs), out_shape=out, in...]
    slice x0 -> x1, local copies, waits for them, and re-layouts: none -> 0.72 us  [local(): return (both[:1], both[1:])]
where the time goes in v5:
time: 41.8 us; the launch traced here: 41.7 us
  Pallas kernels  40.3 us (96%)
  local copies, waits for them, and re-layouts  0.72 us (2%)
  between operations  0.64 us (2%)
    pallas_call x1, Pallas kernels, local(): pl.pallas_call(functools.partial(kernel, views, slabs), out_shape=out, in...  40.3 us

profile of v5, /device:TPU:2, one launch (start us, length us, event | category | flops | bytes accessed | tf_op | source)
XLA Modules:
  0.0 41.7 jit_solution(7071131285927056597)
XLA Ops:
  0.6 40.3 %views.1 = bf16[2,4,128,128]{3,2,1,0:T(8,128)(2,1)S(1)} custom-call(bf16[1,4,128,128]{3,2,1,0:T(8,128)(2,1)} %feat.1, bf16[3,3,128,128]{3,2,1,0:T(8,128)(2,1)} %conv_w.1, bf16[128,128]{1,0:T(8,128)(2,1)} %q_w.1, bf16[128,128]{1,0:T(8,128)(2,1)} %k_w.1, bf16[128,128]{1,0:T(8,128)(2,1)} %v_w.1, s32[2,32]{1,0:T(2,128)} %bitcast.4, s32[2,32]{1,0:T(2,128)} %bitcast.5, ...), custom_call_target="tpu_custom_call" | custom-call | tf_op jit(solution)/shard_map/views/pallas_call | solution.py:404
  41.0 0.7 %fusion = (bf16[1,4,128,128]{3,2,1,0:T(8,128)(2,1)}, bf16[1,4,128,128]{3,2,1,0:T(8,128)(2,1)}) fusion(bf16[2,4,128,128]{3,2,1,0:T(8,128)(2,1)S(1)} %views.1), kind=kLoop, calls=%fused_computation | loop fusion | bytes 524288 | tf_op jit(solution)/shard_map/slice | solution.py:459

commit v6 on v5

--- a/solution.py
+++ b/solution.py
@@ -116,8 +116,8 @@
             outer,
         ),
         remote(
-            feat.at[0, pl.ds(by_core(1, rows - reach), MARGIN)],
-            fbuf.at[pl.ds(by_core(rows + reach + 1, 0), MARGIN)],
+            feat.at[0, by_core(1, rows - MARGIN)],
+            fbuf.at[by_core(rows + reach + 1, reach - MARGIN)],
             halo_send.at[2],
             halo_recv.at[2],
             outer,
@@ -132,8 +132,8 @@
     )
     edge_row = by_core(MARGIN + rows - 1, MARGIN)
     outer_row = by_core(MARGIN, MARGIN + rows - 1)
-    far_rows = by_core(0, MARGIN + rows)
-    places = [*range(MARGIN + 1, MARGIN + rows - 1), edge_row, outer_row, *[far_rows + k for k in range(MARGIN)]]
+    margin_row = by_core(MARGIN - 1, MARGIN + rows)
+    places = [by_core(MARGIN + 1, MARGIN + 2), by_core(MARGIN + 2, MARGIN + 1), edge_row, outer_row, margin_row]
     n_inner = rows - 1
 
     def near(k):
@@ -206,8 +206,8 @@
     conv(outer_row, 1)
     launch([n_inner])
     halo_outer[1].wait_recv()
-    conv(far_rows, MARGIN)
-    launch(range(n_inner + 1, n_inner + reach))
+    conv(margin_row, 1)
+    launch([n_inner + 1])
     relay(range(1, n_inner))
 
     scale = channels**-0.5
@@ -228,8 +228,21 @@
             wsel[0, r] = jnp.where(gap0 == step, cand[0, r], cand[1, r])
             wsel[1, r] = jnp.where(gap1 == step, cand[2, r], cand[3, r])
 
-    relay(range(n_inner, n_inner + reach))
-    select(range(n_inner))
+    select([0])
+    crossing = [
+        remote(
+            wsel.at[side, places[0]],
+            wsel.at[side, by_core(2 * MARGIN + rows - 1, 0)],
+            m_send.at[2 + side],
+            m_recv.at[2 + side],
+            outer,
+        )
+        for side in range(2)
+    ]
+    for copy in crossing:
+        copy.start()
+    relay(range(n_inner, n_inner + 2))
+    select(range(1, n_inner))
     mine = pl.ds(by_core(rows, MARGIN), MARGIN)
     theirs = pl.ds(by_core(0, MARGIN + rows), MARGIN)
     margins = [
@@ -238,8 +251,8 @@
     ]
     for copy in margins:
         copy.start()
-    select(range(n_inner, n_inner + reach))
-    for copy in margins:
+    select(range(n_inner, n_inner + 2))
+    for copy in (*margins, *crossing):
         copy.wait_recv()
 
     base = slab * rows - MARGIN
@@ -375,9 +388,9 @@
     for copy in halo_outer:
         copy.wait_send()
     halo_inner.wait_send()
-    sent = cand.at[:, pl.ds(0, n_inner + reach)]
+    sent = cand.at[:, pl.ds(0, n_inner + 2)]
     pltpu.make_async_copy(sent, sent, z_send).wait()
-    for copy in (*margins, *back[0], *back[1]):
+    for copy in (*margins, *crossing, *back[0], *back[1]):
         copy.wait_send()
     pltpu.make_async_copy(zin, zin, y_send).wait()
 
@@ -397,7 +410,7 @@
 ):
     _, rows, width, channels = features_in.shape
     block = (width, channels)
-    chunks = rows + MARGIN
+    chunks = rows + 1
     hbm = pl.BlockSpec(memory_space=pl.ANY)
     dma = pltpu.SemaphoreType.DMA
     out = jax.ShapeDtypeStruct((2, *features_in.shape[1:]), BF16)
@@ -431,8 +444,8 @@
             dma((3,)),
             dma,
             dma((4, chunks)),
-            dma((2,)),
-            dma((2,)),
+            dma((4,)),
+            dma((4,)),
             dma((1 + MARGIN,)),
             dma((1 + MARGIN,)),
             dma,

time: 41.8 us -> 41.2 us (0.986)
  Pallas kernels: 40.3 us -> 39.7 us
    pallas_call x1, Pallas kernels: 40.3 us -> 39.7 us  [local(): pl.pallas_call(functools.partial(kernel, views, slabs), out_shape=out, in...]
where the time goes in v6:
time: 41.2 us; the launch traced here: 41 us
  Pallas kernels  39.7 us (96%)
  local copies, waits for them, and re-layouts  0.72 us (2%)
  between operations  0.64 us (2%)
    pallas_call x1, Pallas kernels, local(): pl.pallas_call(functools.partial(kernel, views, slabs), out_shape=out, in...  39.7 us

profile of v6, /device:TPU:2, one launch (start us, length us, event | category | flops | bytes accessed | tf_op | source)
XLA Modules:
  0.0 41.0 jit_solution(15393115649345103723)
XLA Ops:
  0.6 39.7 %views.1 = bf16[2,4,128,128]{3,2,1,0:T(8,128)(2,1)S(1)} custom-call(bf16[1,4,128,128]{3,2,1,0:T(8,128)(2,1)} %feat.1, bf16[3,3,128,128]{3,2,1,0:T(8,128)(2,1)} %conv_w.1, bf16[128,128]{1,0:T(8,128)(2,1)} %q_w.1, bf16[128,128]{1,0:T(8,128)(2,1)} %k_w.1, bf16[128,128]{1,0:T(8,128)(2,1)} %v_w.1, s32[2,32]{1,0:T(2,128)} %bitcast.4, s32[2,32]{1,0:T(2,128)} %bitcast.5, ...), custom_call_target="tpu_custom_call" | custom-call | tf_op jit(solution)/shard_map/views/pallas_call | solution.py:417
  40.3 0.7 %fusion = (bf16[1,4,128,128]{3,2,1,0:T(8,128)(2,1)}, bf16[1,4,128,128]{3,2,1,0:T(8,128)(2,1)}) fusion(bf16[2,4,128,128]{3,2,1,0:T(8,128)(2,1)S(1)} %views.1), kind=kLoop, calls=%fused_computation | loop fusion | bytes 524288 | tf_op jit(solution)/shard_map/slice | solution.py:472

commit v7 on v6

--- a/solution.py
+++ b/solution.py
@@ -55,6 +55,8 @@
     rmar,
     ztot,
     zin,
+    xout,
+    xin,
     load_sem,
     halo_send,
     halo_recv,
@@ -310,60 +312,54 @@
             summed = part if summed is None else summed + part
         return summed.reshape(count, 2, BLOCK, channels)
 
-    back = [
-        [remote(gmar.at[0], rmar.at[0], b_send.at[0], b_recv.at[0], inner)],
-        [remote(gmar.at[1, i], rmar.at[1, i], b_send.at[1 + i], b_recv.at[1 + i], outer) for i in range(MARGIN)],
-    ]
-    for i in range(MARGIN):
-        gmar[1, i] = key_grads(by_core(0, MARGIN + rows) + i, 1)[0].astype(BF16)
-        back[1][i].start()
-    gmar[0] = key_grads(by_core(MARGIN + rows, 0), MARGIN).astype(BF16)
-    back[0][0].start()
-
-    def totals(half, i):
-        k = half * MARGIN + i
+    near_half = by_core(MARGIN, 0)
+    own_rows = [None, near_half, near_half + 1, by_core(1, rows - MARGIN), by_core(0, rows - 1)]
+    back_inner = remote(gmar.at[pl.ds(0, MARGIN)], rmar.at[pl.ds(0, MARGIN)], b_send.at[0], b_recv.at[0], inner)
+    back_outer = remote(gmar.at[MARGIN], rmar.at[MARGIN], b_send.at[1], b_recv.at[1], outer)
+    back_cross = remote(xout, xin, b_send.at[2], b_recv.at[2], outer)
+
+    def totals(k):
         return (
             remote(ztot.at[0, k], zin.at[0, k], y_send, y_recv.at[0, k], left),
             remote(ztot.at[1, k], zin.at[1, k], y_send, y_recv.at[1, k], right),
         )
 
-    def relays(half, i):
-        k = half * MARGIN + i
+    def relays(k):
         return (
             remote(zin.at[0, k], zin.at[2, k], y_send, y_recv.at[2, k], left),
             remote(zin.at[1, k], zin.at[3, k], y_send, y_recv.at[3, k], right),
         )
 
-    firsts = (by_core(MARGIN, 0), by_core(0, MARGIN))
-
-    def send_row(half, i, summed):
-        k = half * MARGIN + i
-        ztot[:, k] = (summed[i] + rmar[half, i].astype(F32)).astype(BF16)
-        for copy in totals(half, i):
+    def send_row(k, summed):
+        ztot[:, k] = summed.astype(BF16)
+        for copy in totals(k):
             copy.start()
 
-    def relay_half(half):
-        for i in range(MARGIN):
-            for copy, onward in zip(totals(half, i), relays(half, i)):
-                copy.wait_recv()
-                onward.start()
-
-    first_half = key_grads(MARGIN + firsts[0], MARGIN)
-    back[0][0].wait_recv()
+    def relay_row(k):
+        for copy, onward in zip(totals(k), relays(k)):
+            copy.wait_recv()
+            onward.start()
+
+    gmar[MARGIN] = key_grads(by_core(MARGIN - 1, MARGIN + rows), 1)[0].astype(BF16)
+    back_outer.start()
+    send_row(0, key_grads(by_core(0, 2 * MARGIN + rows - 1), 1)[0])
+    gmar[pl.ds(0, MARGIN)] = key_grads(by_core(MARGIN + rows, 0), MARGIN).astype(BF16)
+    back_inner.start()
+    send_row(3, key_grads(MARGIN + own_rows[3], 1)[0])
+    half = key_grads(MARGIN + near_half, MARGIN)
+    back_inner.wait_recv()
     for i in range(MARGIN):
-        send_row(0, i, first_half)
-    last_half = key_grads(MARGIN + firsts[1], MARGIN)
+        send_row(1 + i, half[i] + rmar[i].astype(F32))
+    last = key_grads(MARGIN + own_rows[4], 1)[0]
     for q in range(rows // 2):
         combine(q)
-    back[1][0].wait_recv()
-    send_row(1, 0, last_half)
-    combine(rows // 2)
-    back[1][1].wait_recv()
-    send_row(1, 1, last_half)
-    relay_half(0)
-    for q in range(rows // 2 + 1, rows):
+    relay_row(0)
+    back_outer.wait_recv()
+    send_row(4, last + rmar[MARGIN].astype(F32))
+    for q in range(rows // 2, rows):
         combine(q)
-    relay_half(1)
+    for k in (3, 1, 2):
+        relay_row(k)
 
     def gap_is(other, side, distance):
         other = lax.rem(other + 2 * views, views)
@@ -376,21 +372,32 @@
         gap_is(cam + 2 * step, 0, 2 * step),
         gap_is(cam - 2 * step, 1, 2 * step),
     )
-    for half in range(2):
-        for i in range(MARGIN):
-            for copy in relays(half, i):
-                copy.wait_recv()
-            summed = own[firsts[half] + i]
-            for source in range(4):
-                summed = summed + jnp.where(use[source] > 0, zin[source, half * MARGIN + i].astype(F32), 0.0)
-            both_out[1, firsts[half] + i] = summed.astype(BF16)
+
+    def arrived(k):
+        for copy in relays(k):
+            copy.wait_recv()
+        summed = None
+        for source in range(4):
+            part = jnp.where(use[source] > 0, zin[source, k].astype(F32), 0.0)
+            summed = part if summed is None else summed + part
+        return summed
+
+    xout[...] = arrived(0).astype(BF16)
+    back_cross.start()
+    relay_row(4)
+    for k in (1, 2):
+        both_out[1, own_rows[k]] = (own[own_rows[k]] + arrived(k)).astype(BF16)
+    inside = own[own_rows[3]] + arrived(3)
+    back_cross.wait_recv()
+    both_out[1, own_rows[3]] = (inside + xin[...].astype(F32)).astype(BF16)
+    both_out[1, own_rows[4]] = (own[own_rows[4]] + arrived(4)).astype(BF16)
 
     for copy in halo_outer:
         copy.wait_send()
     halo_inner.wait_send()
     sent = cand.at[:, pl.ds(0, n_inner + 2)]
     pltpu.make_async_copy(sent, sent, z_send).wait()
-    for copy in (*margins, *crossing, *back[0], *back[1]):
+    for copy in (*margins, *crossing, back_inner, back_outer, back_cross):
         copy.wait_send()
     pltpu.make_async_copy(zin, zin, y_send).wait()
 
@@ -435,10 +442,12 @@
             pltpu.VMEM((rows, 2 * width, channels), BF16),
             pltpu.VMEM((rows, 2 * BAND + 1, BLOCK, 2 * width), BF16),
             pltpu.VMEM((rows, *block), F32),
-            pltpu.VMEM((2, 2, MARGIN, *block), BF16),
-            pltpu.VMEM((2, 2, MARGIN, *block), BF16),
-            pltpu.VMEM((2, rows, *block), BF16),
-            pltpu.VMEM((4, rows, *block), BF16),
+            pltpu.VMEM((MARGIN + 1, 2, *block), BF16),
+            pltpu.VMEM((MARGIN + 1, 2, *block), BF16),
+            pltpu.VMEM((2, chunks, *block), BF16),
+            pltpu.VMEM((4, chunks, *block), BF16),
+            pltpu.VMEM(block, BF16),
+            pltpu.VMEM(block, BF16),
             dma((9,)),
             dma((3,)),
             dma((3,)),
@@ -446,10 +455,10 @@
             dma((4, chunks)),
             dma((4,)),
             dma((4,)),
-            dma((1 + MARGIN,)),
-            dma((1 + MARGIN,)),
+            dma((3,)),
+            dma((3,)),
             dma,
-            dma((4, rows)),
+            dma((4, chunks)),
         ],
         compiler_params=pltpu.CompilerParams(collective_id=0, has_side_effects=True, vmem_limit_bytes=32 << 20),
         name="views",

time: 41.2 us -> 40 us (0.971)
  the two profiles are of different devices: /device:TPU:2 before, /device:TPU:1 now
where the time goes in v7:
time: 40 us; the launch traced here: 39.8 us
  Pallas kernels  38.5 us (96%)
  local copies, waits for them, and re-layouts  0.72 us (2%)
  between operations  0.64 us (2%)
    pallas_call x1, Pallas kernels, local(): pl.pallas_call(functools.partial(kernel, views, slabs), out_shape=out, in...  38.5 us

profile of v7, /device:TPU:1, one launch (start us, length us, event | category | flops | bytes accessed | tf_op | source)
XLA Modules:
  0.0 39.8 jit_solution(9679417515343058251)
XLA Ops:
  0.6 38.5 %views.1 = bf16[2,4,128,128]{3,2,1,0:T(8,128)(2,1)S(1)} custom-call(bf16[1,4,128,128]{3,2,1,0:T(8,128)(2,1)} %feat.1, bf16[3,3,128,128]{3,2,1,0:T(8,128)(2,1)} %conv_w.1, bf16[128,128]{1,0:T(8,128)(2,1)} %q_w.1, bf16[128,128]{1,0:T(8,128)(2,1)} %k_w.1, bf16[128,128]{1,0:T(8,128)(2,1)} %v_w.1, s32[2,32]{1,0:T(2,128)} %bitcast.4, s32[2,32]{1,0:T(2,128)} %bitcast.5, ...), custom_call_target="tpu_custom_call" | custom-call | tf_op jit(solution)/shard_map/views/pallas_call | solution.py:424
  39.1 0.7 %fusion = (bf16[1,4,128,128]{3,2,1,0:T(8,128)(2,1)}, bf16[1,4,128,128]{3,2,1,0:T(8,128)(2,1)}) fusion(bf16[2,4,128,128]{3,2,1,0:T(8,128)(2,1)S(1)} %views.1), kind=kLoop, calls=%fused_computation | loop fusion | bytes 524288 | tf_op jit(solution)/shard_map/slice | solution.py:481

commit v8 on v7

--- a/solution.py
+++ b/solution.py
@@ -58,13 +58,11 @@
     xout,
     xin,
     load_sem,
-    halo_send,
+    o_send,
     halo_recv,
     z_send,
     z_recv,
-    m_send,
     m_recv,
-    b_send,
     b_recv,
     y_send,
     y_recv,
@@ -113,14 +111,14 @@
         remote(
             feat.at[0, by_core(0, rows - 1)],
             fbuf.at[by_core(rows + reach, reach - 1)],
-            halo_send.at[0],
+            o_send,
             halo_recv.at[0],
             outer,
         ),
         remote(
             feat.at[0, by_core(1, rows - MARGIN)],
             fbuf.at[by_core(rows + reach + 1, reach - MARGIN)],
-            halo_send.at[2],
+            o_send,
             halo_recv.at[2],
             outer,
         ),
@@ -128,7 +126,7 @@
     halo_inner = remote(
         feat.at[0, by_core(rows - 1, 0)],
         fbuf.at[by_core(reach - 1, rows + reach)],
-        halo_send.at[1],
+        o_send,
         halo_recv.at[1],
         inner,
     )
@@ -235,7 +233,7 @@
         remote(
             wsel.at[side, places[0]],
             wsel.at[side, by_core(2 * MARGIN + rows - 1, 0)],
-            m_send.at[2 + side],
+            o_send,
             m_recv.at[2 + side],
             outer,
         )
@@ -248,7 +246,7 @@
     mine = pl.ds(by_core(rows, MARGIN), MARGIN)
     theirs = pl.ds(by_core(0, MARGIN + rows), MARGIN)
     margins = [
-        remote(wsel.at[side, mine], wsel.at[side, theirs], m_send.at[side], m_recv.at[side], inner)
+        remote(wsel.at[side, mine], wsel.at[side, theirs], o_send, m_recv.at[side], inner)
         for side in range(2)
     ]
     for copy in margins:
@@ -314,9 +312,9 @@
 
     near_half = by_core(MARGIN, 0)
     own_rows = [None, near_half, near_half + 1, by_core(1, rows - MARGIN), by_core(0, rows - 1)]
-    back_inner = remote(gmar.at[pl.ds(0, MARGIN)], rmar.at[pl.ds(0, MARGIN)], b_send.at[0], b_recv.at[0], inner)
-    back_outer = remote(gmar.at[MARGIN], rmar.at[MARGIN], b_send.at[1], b_recv.at[1], outer)
-    back_cross = remote(xout, xin, b_send.at[2], b_recv.at[2], outer)
+    back_inner = remote(gmar.at[pl.ds(0, MARGIN)], rmar.at[pl.ds(0, MARGIN)], o_send, b_recv.at[0], inner)
+    back_outer = remote(gmar.at[MARGIN], rmar.at[MARGIN], o_send, b_recv.at[1], outer)
+    back_cross = remote(xout, xin, o_send, b_recv.at[2], outer)
 
     def totals(k):
         return (
@@ -392,13 +390,10 @@
     both_out[1, own_rows[3]] = (inside + xin[...].astype(F32)).astype(BF16)
     both_out[1, own_rows[4]] = (own[own_rows[4]] + arrived(4)).astype(BF16)
 
-    for copy in halo_outer:
-        copy.wait_send()
-    halo_inner.wait_send()
+    others = cand.at[:, pl.ds(0, rows)]
+    pltpu.make_async_copy(others, others, o_send).wait()
     sent = cand.at[:, pl.ds(0, n_inner + 2)]
     pltpu.make_async_copy(sent, sent, z_send).wait()
-    for copy in (*margins, *crossing, back_inner, back_outer, back_cross):
-        copy.wait_send()
     pltpu.make_async_copy(zin, zin, y_send).wait()
 
 
@@ -449,13 +444,11 @@
             pltpu.VMEM(block, BF16),
             pltpu.VMEM(block, BF16),
             dma((9,)),
-            dma((3,)),
+            dma,
             dma((3,)),
             dma,
             dma((4, chunks)),
             dma((4,)),
-            dma((4,)),
-            dma((3,)),
             dma((3,)),
             dma,
             dma((4, chunks)),

time: 40 us -> 39.9 us (level)
  no operation moved by 1% of the time
where the time goes in v8:
time: 39.9 us; the launch traced here: 39.7 us
  Pallas kernels  38.4 us (96%)
  local copies, waits for them, and re-layouts  0.72 us (2%)
  between operations  0.64 us (2%)
    pallas_call x1, Pallas kernels, local(): pl.pallas_call(functools.partial(kernel, views, slabs), out_shape=out, in...  38.4 us

profile of v8, /device:TPU:1, one launch (start us, length us, event | category | flops | bytes accessed | tf_op | source)
XLA Modules:
  0.0 39.7 jit_solution(18057110465224398133)
XLA Ops:
  0.6 38.4 %views.1 = bf16[2,4,128,128]{3,2,1,0:T(8,128)(2,1)S(1)} custom-call(bf16[1,4,128,128]{3,2,1,0:T(8,128)(2,1)} %feat.1, bf16[3,3,128,128]{3,2,1,0:T(8,128)(2,1)} %conv_w.1, bf16[128,128]{1,0:T(8,128)(2,1)} %q_w.1, bf16[128,128]{1,0:T(8,128)(2,1)} %k_w.1, bf16[128,128]{1,0:T(8,128)(2,1)} %v_w.1, s32[2,32]{1,0:T(2,128)} %bitcast.4, s32[2,32]{1,0:T(2,128)} %bitcast.5, ...), custom_call_target="tpu_custom_call" | custom-call | tf_op jit(solution)/shard_map/views/pallas_call | solution.py:419
  39.0 0.7 %fusion = (bf16[1,4,128,128]{3,2,1,0:T(8,128)(2,1)}, bf16[1,4,128,128]{3,2,1,0:T(8,128)(2,1)}) fusion(bf16[2,4,128,128]{3,2,1,0:T(8,128)(2,1)S(1)} %views.1), kind=kLoop, calls=%fused_computation | loop fusion | bytes 524288 | tf_op jit(solution)/shard_map/slice | solution.py:474

commit v9 on v8

--- a/solution.py
+++ b/solution.py
@@ -338,9 +338,9 @@
             copy.wait_recv()
             onward.start()
 
+    send_row(0, key_grads(by_core(0, 2 * MARGIN + rows - 1), 1)[0])
     gmar[MARGIN] = key_grads(by_core(MARGIN - 1, MARGIN + rows), 1)[0].astype(BF16)
     back_outer.start()
-    send_row(0, key_grads(by_core(0, 2 * MARGIN + rows - 1), 1)[0])
     gmar[pl.ds(0, MARGIN)] = key_grads(by_core(MARGIN + rows, 0), MARGIN).astype(BF16)
     back_inner.start()
     send_row(3, key_grads(MARGIN + own_rows[3], 1)[0])

time: 39.9 us -> 39.9 us (level)
  no operation moved by 1% of the time
where the time goes in v9:
time: 39.9 us; the launch traced here: 39.7 us
  Pallas kernels  38.4 us (96%)
  local copies, waits for them, and re-layouts  0.72 us (2%)
  between operations  0.64 us (2%)
    pallas_call x1, Pallas kernels, local(): pl.pallas_call(functools.partial(kernel, views, slabs), out_shape=out, in...  38.4 us

profile of v9, /device:TPU:1, one launch (start us, length us, event | category | flops | bytes accessed | tf_op | source)
XLA Modules:
  0.0 39.7 jit_solution(10842273986754206180)
XLA Ops:
  0.6 38.4 %views.1 = bf16[2,4,128,128]{3,2,1,0:T(8,128)(2,1)S(1)} custom-call(bf16[1,4,128,128]{3,2,1,0:T(8,128)(2,1)} %feat.1, bf16[3,3,128,128]{3,2,1,0:T(8,128)(2,1)} %conv_w.1, bf16[128,128]{1,0:T(8,128)(2,1)} %q_w.1, bf16[128,128]{1,0:T(8,128)(2,1)} %k_w.1, bf16[128,128]{1,0:T(8,128)(2,1)} %v_w.1, s32[2,32]{1,0:T(2,128)} %bitcast.4, s32[2,32]{1,0:T(2,128)} %bitcast.5, ...), custom_call_target="tpu_custom_call" | custom-call | tf_op jit(solution)/shard_map/views/pallas_call | solution.py:419
  39.0 0.7 %fusion = (bf16[1,4,128,128]{3,2,1,0:T(8,128)(2,1)}, bf16[1,4,128,128]{3,2,1,0:T(8,128)(2,1)}) fusion(bf16[2,4,128,128]{3,2,1,0:T(8,128)(2,1)S(1)} %views.1), kind=kLoop, calls=%fused_computation | loop fusion | bytes 524288 | tf_op jit(solution)/shard_map/slice | solution.py:474
